TPU v7x, 128 devices: a whole 4x4x4 slice. The times are simulated.
128 devices in a mesh: dp: 8 (over y_hi, x), row: 4 (over z), col: 4 (over y_lo, core).
Axes of the slice: x: 4, y: 4 (y_hi: 2, y_lo: 2; y = y_hi * 2 + y_lo), z: 4, core: 2. Of those that a mesh axis runs over, the one named last changes fastest.
Arguments:
- tokens: bfloat16 [8192, 2048], P(('dp', 'col'), 'row'), may hold values from -6 to 6
- documents: int32 [8, 1024], P('dp'), may hold values from 0 to 3, never falling along the last dimension, each value on 1 to 512 neighbouring positions
- piece_starts: int32 [8, 2], P('dp'), may hold values from 0 to 768, as said below
- latent_down: bfloat16 [2048, 1024], P('row'), may hold values from -0.125 to 0.125
- key_value: bfloat16 [2048, 512], P('row'), may hold values from -0.125 to 0.125
- query_up: bfloat16 [1024, 4096], P(None, 'row'), may hold values from -0.1875 to 0.1875
- output_weight: bfloat16 [4096, 2048], P('row', 'col'), may hold values from -0.75 to 0.75
- gate_weight: bfloat16 [2048, 5632], P('row', 'col'), may hold values from -0.125 to 0.125
- up_weight: bfloat16 [2048, 5632], P('row', 'col'), may hold values from -0.125 to 0.125
- down_weight: bfloat16 [5632, 2048], P('col', 'row'), may hold values from -0.15625 to 0.15625
- input_gain: float32 [2048], P('row'), may hold values from 0.5 to 1.5
- latent_gain: float32 [1024], replicated, may hold values from 0.5 to 1.5
- middle_gain: float32 [2048], P('row'), may hold values from 0.5 to 1.5
- cotangent: bfloat16 [8192, 2048], P(('dp', 'col'), 'row'), may hold values from -6 to 6
Outputs:
- layer_out: bfloat16 [8192, 2048], P(('dp', 'col'), 'row')
- grad_tokens: bfloat16 [8192, 2048], P(('dp', 'col'), 'row')
- grad_latent_down: float32 [2048, 1024], P('row')
- grad_key_value: float32 [2048, 512], P('row')
- grad_query_up: float32 [1024, 4096], P(None, 'row')
- grad_output_weight: float32 [4096, 2048], P('row', 'col')
- grad_gate_weight: float32 [2048, 5632], P('row', 'col')
- grad_up_weight: float32 [2048, 5632], P('row', 'col')
- grad_down_weight: float32 [5632, 2048], P('col', 'row')
- grad_input_gain: float32 [2048], P('row')
- grad_latent_gain: float32 [1024], replicated
- grad_middle_gain: float32 [2048], P('row')
Inputs may be any that keep to these rules, and one draw needn't show every extreme that they name: `documents`: within each sequence the document numbers never fall; each document has 1 to 512 tokens. `piece_starts`: piece m of a sequence starts in the m-th of 2 equal zones of the sequence and ends inside that zone; the first sequence has a piece at its start and one at its end.
All inputs are finite; a program needn't handle non-finite values.
Results may differ from a plain program's by a relative error of at most 0.033.
Values may be sent and summed in bfloat16 or wider, within the bound.
A program may use at most 128 MiB of HBM per device.

v0:
```python
import math

import jax
import jax.numpy as jnp
from jax import lax
from jax.sharding import PartitionSpec as P

D = 2048
SEQ = 1024
PIECE = 256


epsilon = 1e-06
masked_value = -1e30


def copy_for_each(array, axis):
    size = lax.axis_size(axis)
    return lax.all_to_all(
        jnp.broadcast_to(array[None], (size, *array.shape)), axis, 0, 0, tiled=True
    )


def of_everyone(array, axis):
    everything = copy_for_each(array, axis)
    return jnp.sum(everything, axis=0)


def in_order(parts, dim):
    dims = list(parts.shape[1:])
    dims[dim] *= parts.shape[0]
    return jnp.moveaxis(parts, 0, dim).reshape(dims)


def gathered_copies(array, axis, dim):
    return in_order(copy_for_each(array, axis), dim)


def in_blocks(array, dim, size):
    before, after = (array.shape[:dim], array.shape[dim + 1 :])
    return jnp.moveaxis(array.reshape(*before, size, -1, *after), dim, 0)


def summed_on_arrival(array, axis, dim):
    size = lax.axis_size(axis)
    parts = lax.all_to_all(in_blocks(array, dim, size), axis, 0, 0, tiled=True)
    return jnp.sum(parts.astype(jnp.float32), axis=0)


def rope_tables(positions, width):
    half_width = width // 2
    frequency = jnp.exp(-math.log(10000.0) * jnp.arange(half_width, dtype=jnp.float32) / half_width)
    angles = positions.astype(jnp.float32)[:, None] * frequency[None, :]
    cosine = jnp.cos(angles)
    sine_part = jnp.sin(angles)
    return (
        jnp.concatenate([cosine, cosine], axis=1),
        jnp.concatenate([sine_part, sine_part], axis=1),
    )


def rotate(values, cosine, sine_part):
    half_width = values.shape[-1] // 2
    turned = jnp.concatenate([-values[..., half_width:], values[..., :half_width]], axis=-1)
    return values * cosine + turned * sine_part


def unrotate(grads_in, cosine, sine_part):
    half_width = grads_in.shape[-1] // 2
    scaled = grads_in * sine_part
    turned = jnp.concatenate([scaled[..., half_width:], -scaled[..., :half_width]], axis=-1)
    return grads_in * cosine + turned


def piece_labels(positions, starts_row):
    inside = (positions[:, None] >= starts_row[None, :]) & (
        positions[:, None] < starts_row[None, :] + PIECE
    )
    numbers = jnp.arange(1, starts_row.shape[0] + 1, dtype=jnp.int32)
    return jnp.sum(jnp.where(inside, numbers[None, :], 0), axis=1) - 1


def allowed(query_place, key_place, query_doc, key_doc, starts_row):
    query_piece = piece_labels(query_place, starts_row)
    key_piece = piece_labels(key_place, starts_row)
    same_doc = query_doc[:, None] == key_doc[None, :]
    causal = key_place[None, :] <= query_place[:, None]
    same_piece = (query_piece[:, None] == key_piece[None, :]) & (query_piece[:, None] >= 0)
    return same_doc & (causal | same_piece)


def shards(
    tokens,
    documents,
    piece_starts,
    latent_down,
    key_value,
    query_up,
    output_weight,
    gate_weight,
    up_weight,
    down_weight,
    input_gain,
    latent_gain,
    middle_gain,
    cotangent,
):
    local_rows = tokens.shape[0]
    group_rows = local_rows * lax.axis_size("col")
    row_share = group_rows // lax.axis_size("row")
    latent_width = latent_down.shape[1]
    head_dim = key_value.shape[1] // 2
    local_heads = query_up.shape[1] // head_dim
    ffn_local = gate_weight.shape[1]
    score_scale = 1.0 / math.sqrt(head_dim)
    col_first = lax.axis_index("col") * local_rows
    own_places = (col_first + jnp.arange(local_rows, dtype=jnp.int32)) % SEQ
    own_cos, own_sin = rope_tables(own_places, head_dim)

    def feature_sum(values):
        return of_everyone(values, "row")

    def along_cols(values):
        return gathered_copies(values, "col", 0)

    def along_rows(values):
        return lax.all_gather(values, "row", axis=0, tiled=True)

    def sum_to_cols(term_fn):
        return lax.psum_scatter(
            term_fn(jnp.int32(0), local_rows * lax.axis_size("col")).astype(jnp.bfloat16),
            "col",
            scatter_dimension=0,
            tiled=True,
        ).astype(jnp.float32)

    def sum_to_rows(term_fn):
        return lax.psum_scatter(
            term_fn(jnp.int32(0), row_share * lax.axis_size("row")).astype(jnp.bfloat16),
            "row",
            scatter_dimension=0,
            tiled=True,
        ).astype(jnp.float32)

    def over_heads(first_part, second_part):
        return lax.psum((first_part, second_part), "row")

    inputs = tokens.astype(jnp.float32)
    scale_in = lax.rsqrt(feature_sum(jnp.sum(inputs * inputs, axis=1)) / D + epsilon)
    normed = (inputs * scale_in[:, None] * input_gain).astype(jnp.bfloat16)
    latent, pair_own = over_heads(
        jnp.dot(normed, latent_down, preferred_element_type=jnp.float32),
        jnp.dot(normed, key_value, preferred_element_type=jnp.float32),
    )
    keys_own = rotate(pair_own[:, :head_dim], own_cos, own_sin).astype(jnp.bfloat16)
    pair_sent = along_cols(
        jnp.concatenate([keys_own, pair_own[:, head_dim:].astype(jnp.bfloat16)], axis=1)
    )
    keys_all = pair_sent[:, :head_dim]
    values_all = pair_sent[:, head_dim:]
    latent_scale = lax.rsqrt(jnp.mean(latent * latent, axis=1) + epsilon)
    latent_normed = (latent * latent_scale[:, None] * latent_gain).astype(jnp.bfloat16)
    query_raw = jnp.dot(latent_normed, query_up, preferred_element_type=jnp.float32).reshape(
        local_rows, local_heads, head_dim
    )
    queries = rotate(query_raw, own_cos[:, None, :], own_sin[:, None, :]).astype(jnp.bfloat16)
    block_rows = min(local_rows, SEQ)

    def block_setup(block_index):
        begin_at = col_first + block_index * block_rows
        seq_index = begin_at // SEQ
        query_place = begin_at % SEQ + jnp.arange(block_rows, dtype=jnp.int32)
        key_place = jnp.arange(SEQ, dtype=jnp.int32)
        doc_row = lax.dynamic_index_in_dim(documents, seq_index, 0, keepdims=False)
        starts_row = lax.dynamic_index_in_dim(piece_starts, seq_index, 0, keepdims=False)
        query_doc = lax.dynamic_slice_in_dim(doc_row, begin_at % SEQ, block_rows, 0)
        allowed_pairs = allowed(query_place, key_place, query_doc, doc_row, starts_row)
        raw_scores = (
            jnp.einsum("qhd,kd->qhk", queries, keys_all, preferred_element_type=jnp.float32)
            * score_scale
        )
        scores = jnp.where(allowed_pairs[:, None, :], raw_scores, masked_value)
        return (seq_index, keys_all, values_all, queries, scores)

    block_index = 0
    seq_index, keys_block, values_block, query_block, scores = block_setup(block_index)
    top_score = jnp.max(scores, axis=2, keepdims=True)
    weights_raw = jnp.exp(scores - top_score)
    totals = jnp.sum(weights_raw, axis=2, keepdims=True)
    weights_low = (weights_raw / totals).astype(jnp.bfloat16)
    mixed_blocks = jnp.einsum(
        "qhk,kd->qhd", weights_low, values_block, preferred_element_type=jnp.float32
    )
    lse_blocks = [top_score + jnp.log(totals)]
    mixed_heads = mixed_blocks.reshape(local_rows, local_heads * head_dim).astype(jnp.bfloat16)
    output_all = lax.all_gather(output_weight, "col", axis=1, tiled=True)
    branch = summed_on_arrival(
        jnp.dot(mixed_heads, output_all, preferred_element_type=jnp.float32).astype(jnp.bfloat16),
        "row",
        1,
    )
    middle = inputs + branch
    scale_mid = lax.rsqrt(feature_sum(jnp.sum(middle * middle, axis=1)) / D + epsilon)
    normed_mid = (middle * scale_mid[:, None] * middle_gain).astype(jnp.bfloat16)
    normed_mid_all = along_cols(normed_mid)
    gate_up = jnp.concatenate([gate_weight, up_weight], axis=1)

    def gate_term(begin_at, row_count):
        return jnp.dot(normed_mid_all, gate_up, preferred_element_type=jnp.float32)

    summed = sum_to_rows(gate_term)
    gate_val = summed[:, :ffn_local]
    up_val = summed[:, ffn_local:]
    sigmoid_gate = jax.nn.sigmoid(gate_val)
    silu_gate = gate_val * sigmoid_gate
    activated = (silu_gate * up_val).astype(jnp.bfloat16)
    activated_all = along_rows(activated)

    def down_term(begin_at, row_count):
        return jnp.dot(activated_all, down_weight, preferred_element_type=jnp.float32)

    feed_out = sum_to_cols(down_term)
    layer_out = (middle + feed_out).astype(jnp.bfloat16)
    upstream_all = along_cols(cotangent)

    def act_grad_term(begin_at, row_count):
        return jnp.dot(upstream_all, down_weight.T, preferred_element_type=jnp.float32)

    grad_act = sum_to_rows(act_grad_term)
    grad_down = jnp.dot(activated_all.T, upstream_all, preferred_element_type=jnp.float32)
    grad_up_val = grad_act * silu_gate
    grad_gate_val = grad_act * up_val * sigmoid_gate * (1.0 + gate_val * (1.0 - sigmoid_gate))
    grad_pair = jnp.concatenate([grad_gate_val, grad_up_val], axis=1).astype(jnp.bfloat16)
    grad_pair_all = along_rows(grad_pair)

    def mid_grad_term(begin_at, row_count):
        return jnp.dot(grad_pair_all, gate_up.T, preferred_element_type=jnp.float32)

    grad_normed_mid = sum_to_cols(mid_grad_term)
    grad_gate_up = jnp.dot(normed_mid_all.T, grad_pair_all, preferred_element_type=jnp.float32)
    grad_gate = grad_gate_up[:, :ffn_local]
    grad_up = grad_gate_up[:, ffn_local:]
    gained_mid = grad_normed_mid * middle_gain
    stat_mid = feature_sum(jnp.sum(gained_mid * middle, axis=1))
    grad_middle = (
        cotangent.astype(jnp.float32)
        + scale_mid[:, None] * gained_mid
        - middle * (scale_mid**3 * stat_mid / D)[:, None]
    )
    grad_mid_gain = jnp.sum(grad_normed_mid * middle * scale_mid[:, None], axis=0)
    grad_branch = grad_middle.astype(jnp.bfloat16)
    grad_branch_all = gathered_copies(grad_branch, "row", 1)
    grad_mixed = jnp.dot(grad_branch_all, output_all.T, preferred_element_type=jnp.float32).astype(
        jnp.bfloat16
    )
    grad_mixed = grad_mixed.reshape(local_rows, local_heads, head_dim)
    grad_output_all = jnp.dot(mixed_heads.T, grad_branch_all, preferred_element_type=jnp.float32)
    grad_output = lax.psum_scatter(
        grad_output_all.astype(jnp.bfloat16), "col", scatter_dimension=1, tiled=True
    ).astype(jnp.float32)
    grad_keys_all = jnp.zeros((group_rows, 2 * head_dim), jnp.float32)
    block_index = 0
    seq_index, keys_block, values_block, query_block, scores = block_setup(block_index)
    weights_exact = jnp.exp(scores - lse_blocks[block_index])
    weights_low = weights_exact.astype(jnp.bfloat16)
    grad_weights = jnp.einsum(
        "qhd,kd->qhk", grad_mixed, values_block, preferred_element_type=jnp.float32
    )
    row_dot = jnp.sum(grad_weights * weights_exact, axis=2, keepdims=True)
    grad_scores = (weights_exact * (grad_weights - row_dot)).astype(jnp.bfloat16)
    grad_query_blocks = score_scale * jnp.einsum(
        "qhk,kd->qhd", grad_scores, keys_block, preferred_element_type=jnp.float32
    )
    grad_key_block = score_scale * jnp.einsum(
        "qhk,qhd->kd", grad_scores, query_block, preferred_element_type=jnp.float32
    )
    grad_value_block = jnp.einsum(
        "qhk,qhd->kd", weights_low, grad_mixed, preferred_element_type=jnp.float32
    )
    update = jnp.concatenate([grad_key_block, grad_value_block], axis=1)
    grad_keys_all = update
    grad_query_raw = (
        unrotate(grad_query_blocks, own_cos[:, None, :], own_sin[:, None, :])
        .reshape(local_rows, local_heads * head_dim)
        .astype(jnp.bfloat16)
    )
    grad_query_up = jnp.dot(latent_normed.T, grad_query_raw, preferred_element_type=jnp.float32)

    def pair_term(begin_at, row_count):
        return grad_keys_all

    grad_latent_normed, grad_pair_own = over_heads(
        jnp.dot(grad_query_raw, query_up.T, preferred_element_type=jnp.float32),
        sum_to_cols(pair_term),
    )
    grad_keys_raw = unrotate(grad_pair_own[:, :head_dim], own_cos, own_sin)
    gained_latent = grad_latent_normed * latent_gain
    grad_latent = (
        latent_scale[:, None] * gained_latent
        - latent * (latent_scale**3 * jnp.mean(gained_latent * latent, axis=1))[:, None]
    )
    grad_latent_gain = jnp.sum(grad_latent_normed * latent * latent_scale[:, None], axis=0)
    grad_lat = jnp.concatenate(
        [grad_latent, grad_keys_raw, grad_pair_own[:, head_dim:]], axis=1
    ).astype(jnp.bfloat16)
    grad_latent_down = jnp.dot(
        normed.T, grad_lat[:, :latent_width], preferred_element_type=jnp.float32
    )
    grad_key_value = jnp.dot(
        normed.T, grad_lat[:, latent_width:], preferred_element_type=jnp.float32
    )
    grad_normed = jnp.dot(
        grad_lat[:, :latent_width], latent_down.T, preferred_element_type=jnp.float32
    )
    grad_normed = grad_normed + jnp.dot(
        grad_lat[:, latent_width:], key_value.T, preferred_element_type=jnp.float32
    )
    gained_in = grad_normed * input_gain
    stat_in = feature_sum(jnp.sum(gained_in * inputs, axis=1))
    grad_inputs = (
        grad_middle + scale_in[:, None] * gained_in - inputs * (scale_in**3 * stat_in / D)[:, None]
    )
    grad_input_gain = jnp.sum(grad_normed * inputs * scale_in[:, None], axis=0)
    shared = (
        lax.psum(grad_latent_down.astype(jnp.bfloat16), ("dp", "col")).astype(jnp.float32),
        lax.psum(grad_key_value.astype(jnp.bfloat16), ("dp", "col")).astype(jnp.float32),
        lax.psum(grad_query_up.astype(jnp.bfloat16), ("dp", "col")).astype(jnp.float32),
        lax.psum(grad_input_gain.astype(jnp.bfloat16), ("dp", "col")).astype(jnp.float32),
        lax.psum(grad_latent_gain.astype(jnp.bfloat16), ("dp", "col")).astype(jnp.float32),
        lax.psum(grad_mid_gain.astype(jnp.bfloat16), ("dp", "col")).astype(jnp.float32),
    )
    grad_output, grad_gate, grad_up, grad_down = (
        lax.psum(grad_output.astype(jnp.bfloat16), "dp").astype(jnp.float32),
        lax.psum(grad_gate.astype(jnp.bfloat16), "dp").astype(jnp.float32),
        lax.psum(grad_up.astype(jnp.bfloat16), "dp").astype(jnp.float32),
        lax.psum(grad_down.astype(jnp.bfloat16), "dp").astype(jnp.float32),
    )
    return (
        layer_out,
        grad_inputs.astype(jnp.bfloat16),
        shared[0],
        shared[1],
        shared[2],
        grad_output,
        grad_gate,
        grad_up,
        grad_down,
        shared[3],
        shared[4],
        shared[5],
    )


def solution(mesh):
    placed = (
        P(("dp", "col"), "row"),
        P("dp", None),
        P("dp", None),
        P("row", None),
        P("row", None),
        P(None, "row"),
        P("row", "col"),
        P("row", "col"),
        P("row", "col"),
        P("col", "row"),
        P("row"),
        P(),
        P("row"),
        P(("dp", "col"), "row"),
    )
    return jax.shard_map(
        shards,
        mesh=mesh,
        in_specs=placed,
        out_specs=(
            P(("dp", "col"), "row"),
            P(("dp", "col"), "row"),
            P("row", None),
            P("row", None),
            P(None, "row"),
            P("row", "col"),
            P("row", "col"),
            P("row", "col"),
            P("col", "row"),
            P("row"),
            P(),
            P("row"),
        ),
        check_vma=False,
    )
```

profile of v0, /device:TPU:1, one launch (start us, length us, event | category | flops | bytes accessed | tf_op | source)
XLA Modules:
  0.0 785.6 jit_solution(8894601632923249674)
XLA Ops:
  9.4 9.8 %all_to_all.49 = f32[4,1,256]{2,1,0:T(1,128)S(1)} all-to-all(f32[4,1,256]{2,1,0:T(1,128)S(1)} %broadcast_in_dim.69), channel_id=1, replica_groups=mesh['dp'=8,'row'=4,'col'=4] {'row'}, dimensions={0} | all-to-all | bytes 8192 | tf_op jit(solution)/shard_map/all_to_all | solution.py:19
  19.2 2.8 fusion.63
  22.0 2.1 fusion.61
  26.8 49.2 %all-reduce.12.cloned.1.call-done = (f32[256,1024]{1,0:T(8,128)}, f32[256,512]{1,0:T(8,128)}) async-done(((f32[256,1024]{1,0:T(8,128)}, f32[256,512]{1,0:T(8,128)}), (f32[256,1024]{1,0:T(8,128)}, f32[256,512]{1,0:T(8,128)})) %all-reduce.12.cloned.1.call-update) | async-done | bytes 1572880 | tf_op jit(solution)/shard_map/psum | solution.py:146
  85.6 5.0 all-to-all-start.1
  93.6 10.8 %all-to-all-done.1 = bf16[4,256,512]{2,1,0:T(8,128)(2,1)} async-done(((bf16[4,256,512]{2,1,0:T(8,128)(2,1)}), bf16[4,256,512]{2,1,0:T(8,128)(2,1)}, u32[]{:S(2)}, u32[]{:S(2)}) %all-to-all-start.1) | async-done | bytes 1048608 | tf_op jit(solution)/shard_map/all_to_all | solution.py:19
  104.4 2.3 fusion.68
  108.7 3.1 fusion.19
  111.8 3.6 convolution_convert_fusion.5
  115.5 16.5 %all_to_all.50 = bf16[4,256,512]{2,1,0:T(8,128)(2,1)S(1)} all-to-all(bf16[4,256,512]{2,1,0:T(8,128)(2,1)S(1)} %bitcast.86), channel_id=1, replica_groups=mesh['dp'=8,'row'=4,'col'=4] {'row'}, dimensions={0} | all-to-all | bytes 2097152 | tf_op jit(solution)/shard_map/all_to_all | solution.py:46
  133.0 7.1 all_to_all.51
  144.3 7.5 all-to-all-start.4
  152.0 2.7 constant_dynamic-update-slice_fusion.1
  155.8 9.6 %all-to-all-done.4 = bf16[4,256,512]{2,1,0:T(8,128)(2,1)} async-done(((bf16[4,256,512]{2,1,0:T(8,128)(2,1)}), bf16[4,256,512]{2,1,0:T(8,128)(2,1)}, u32[]{:S(2)}, u32[]{:S(2)}) %all-to-all-start.4) | async-done | bytes 1048608 | tf_op jit(solution)/shard_map/all_to_all | solution.py:19
  165.5 7.8 convolution_convert_fusion
  174.5 17.1 %all_to_all.52 = bf16[4,256,512]{2,1,0:T(8,128)(2,1)S(1)} all-to-all(bf16[4,256,512]{2,1,0:T(8,128)(2,1)S(1)} %broadcast_in_dim.74), channel_id=1, replica_groups=mesh['dp'=8,'row'=4,'col'=4] {'col'}, dimensions={0} | all-to-all | bytes 2097152 | tf_op jit(solution)/shard_map/all_to_all | solution.py:19
  192.6 3.4 convolution_convert_fusion.3
  196.1 36.8 %reduce-scatter.7.cloned.1.call-done = bf16[256,2816]{1,0:T(8,128)(2,1)} async-done(((bf16[1024,2816]{1,0:T(8,128)(2,1)}), bf16[256,2816]{1,0:T(8,128)(2,1)}) %reduce-scatter.7.cloned.1.call-update) | async-done | bytes 1441808 | tf_op jit(solution)/shard_map/reduce_scatter | solution.py:138
  232.9 3.1 convert_element_type.173
  236.0 35.8 %reduce-scatter.11.cloned.1.call-done = bf16[256,1408]{1,0:T(8,128)(2,1)} async-done(((bf16[1024,1408]{1,0:T(8,128)(2,1)}), bf16[256,1408]{1,0:T(8,128)(2,1)}) %reduce-scatter.11.cloned.1.call-update) | async-done | bytes 720912 | tf_op jit(solution)/shard_map/reduce_scatter | solution.py:138
  271.8 3.8 fusion.8
  276.9 61.1 %all-gather.8.cloned.1.call-done = bf16[1024,2816]{1,0:T(8,128)(2,1)} async-done(((bf16[256,2816]{1,0:T(8,128)(2,1)}), bf16[1024,2816]{1,0:T(8,128)(2,1)}) %all-gather.8.cloned.1.call-update) | async-done | bytes 5767184 | tf_op jit(solution)/shard_map/all_gather | solution.py:127
  338.0 7.6 convolution_convert_fusion.7
  346.3 20.6 %reduce-scatter.13.cloned.1.call-done = bf16[256,512]{1,0:T(8,128)(2,1)} async-done(((bf16[1024,512]{1,0:T(8,128)(2,1)}), bf16[256,512]{1,0:T(8,128)(2,1)}) %reduce-scatter.13.cloned.1.call-update) | async-done | bytes 262160 | tf_op jit(solution)/shard_map/reduce_scatter | solution.py:130
  368.8 8.2 %all_to_all.53 = f32[4,1,256]{2,1,0:T(1,128)} all-to-all(f32[4,1,256]{2,1,0:T(1,128)S(1)} %broadcast_in_dim.75), channel_id=1, replica_groups=mesh['dp'=8,'row'=4,'col'=4] {'row'}, dimensions={0} | all-to-all | bytes 8192 | tf_op jit(solution)/shard_map/all_to_all | solution.py:19
  379.6 2.1 fusion.57
  385.4 4.2 all-to-all-start.7
  394.2 9.4 %all-to-all-done.7 = bf16[4,256,512]{1,2,0:T(8,128)(2,1)} async-done(((bf16[4,256,512]{1,2,0:T(8,128)(2,1)}), bf16[4,256,512]{1,2,0:T(8,128)(2,1)}, u32[]{:S(2)}, u32[]{:S(2)}) %all-to-all-start.7) | async-done | bytes 1048608 | tf_op jit(solution)/shard_map/all_to_all | solution.py:19
  403.6 4.6 convolution_convert_fusion.11
  410.2 4.3 multiply_reduce_fusion
  415.5 2.2 broadcast_multiply_fusion
  420.7 2.6 fusion.18
  425.9 4.7 convolution_convert_fusion.2
  430.8 5.0 convolution_convert_fusion.9
  435.8 3.2 convolution_convert_fusion.6
  439.0 26.7 %all-reduce.10.cloned.1.call-done = f32[256,1024]{1,0:T(8,128)} async-done(((f32[256,1024]{1,0:T(8,128)}), f32[256,1024]{1,0:T(8,128)}) %all-reduce.10.cloned.1.call-update) | async-done | bytes 1048592 | tf_op jit(solution)/shard_map/psum | solution.py:146
  465.7 2.1 multiply_reduce_fusion.1
  472.4 19.0 %all-reduce.17 = f32[256,512]{1,0:T(8,128)S(1)} all-reduce(bf16[256,512]{1,0:T(8,128)(2,1)} %reduce-scatter.15.cloned.1.call-done), channel_id=1, replica_groups=mesh['dp'=8,'row'=4,'col'=4] {'row'}, use_global_device_ids=true, to_apply=%region_22.23 | all-reduce | flops 131072 | bytes 786432 | tf_op jit(solution)/shard_map/psum | solution.py:146
  494.1 4.6 convolution_convert_fusion.4
  498.7 6.2 convolution_convert_fusion.1
  509.2 2.6 fusion.39
  512.3 3.2 all-to-all-start.8
  515.6 67.8 %all-reduce.1 = (bf16[512]{0:T(512)(128)(2,1)S(1)}, bf16[1024]{0:T(1024)(128)(2,1)S(1)}, bf16[512]{0:T(512)(128)(2,1)S(1)}) all-reduce(bf16[512]{0:T(512)(128)(2,1)S(1)} %get-tuple-element.16, bf16[1024]{0:T(1024)(128)(2,1)S(1)} %copy-done.44, bf16[512]{0:T(512)(128)(2,1)S(1)} %copy-done.46), channel_id=1, replica_groups=mesh['dp'=8,'row'=4,'col'=4] {'dp','col'}, use_global_device_ids=true, to_apply=%region_34.35 | all-reduce | flops 2048 | bytes 8192 | tf_op jit(solution)/shard_map/psum | solution.py:328
  585.3 2.3 fusion.37
  587.6 47.9 %all-reduce.14.cloned.1.call-done = (bf16[512,1024]{1,0:T(8,128)(2,1)}, bf16[512,512]{1,0:T(8,128)(2,1)}, bf16[1024,1024]{1,0:T(8,128)(2,1)}) async-done(((bf16[512,1024]{1,0:T(8,128)(2,1)}, bf16[512,512]{1,0:T(8,128)(2,1)}, bf16[1024,1024]{1,0:T(8,128)(2,1)}), (bf16[512,1024]{1,0:T(8,128)(2,1)}, bf16[512,512]{1,0:T(8,128)(2,1)}, bf16[1024,1024]{1,0:T(8,128)(2,1)})) %all-reduce.14.cloned.1.call-update) | async-done | bytes 3670032 | tf_op jit(solution)/shard_map/psum | solution.py:325
  635.5 4.2 convert_element_type.196
  642.4 126.6 %all-reduce.16.cloned.1.call-done = (bf16[1024,512]{1,0:T(8,128)(2,1)}, bf16[512,1408]{1,0:T(8,128)(2,1)}, bf16[512,1408]{1,0:T(8,128)(2,1)}, bf16[1408,512]{1,0:T(8,128)(2,1)}) async-done(((bf16[1024,512]{1,0:T(8,128)(2,1)}, bf16[512,1408]{1,0:T(8,128)(2,1)}, bf16[512,1408]{1,0:T(8,128)(2,1)}, bf16[1408,512]{1,0:T(8,128)(2,1)}), (bf16[1024,512]{1,0:T(8,128)(2,1)}, bf16[512,1408]{1,0:T(8,128)(2,1)}, ...) | async-done | bytes 5373968 | tf_op jit(solution)/shard_map/psum | solution.py:333
  769.0 3.2 convert_element_type.199
  (208 shorter events, 72.4 us)
Async XLA Ops:
  8.0 83.4 %copy-start = (bf16[1024,1024]{1,0:T(8,128)(2,1)S(1)}, bf16[1024,1024]{1,0:T(8,128)(2,1)}, u32[]{:S(2)}) copy-start(bf16[1024,1024]{1,0:T(8,128)(2,1)} %param.19) | copy-start | bytes 6291460
  8.0 14.0 %copy-start.11 = (bf16[512,512]{1,0:T(8,128)(2,1)S(1)}, bf16[512,512]{1,0:T(8,128)(2,1)}, u32[]{:S(2)}) copy-start(bf16[512,512]{1,0:T(8,128)(2,1)} %param.18) | copy-start | bytes 1572868
  8.0 68.0 %all-reduce.12.cloned.1.call-start = ((), (), s32[]{:S(2)}) async-start(), calls=%async_computation.25 | async-start | bytes 3145728 | tf_op jit(solution)/shard_map/psum | solution.py:146
  19.2 5.6 copy-start.42
  19.2 5.6 copy-start.45
  19.2 5.6 copy-start.47
  24.1 87.6 %all-gather.4.cloned.1.call-start = ((), (), s32[]{:S(2)}) async-start(), calls=%async_computation.15 | async-start | bytes 5242880 | tf_op jit(solution)/shard_map/all_gather | solution.py:196
  25.6 60.0 %copy-start.16 = (f32[256,128]{1,0:T(8,128)}, f32[256,128]{1,0:T(8,128)S(1)}, u32[]{:S(2)}) copy-start(f32[256,128]{1,0:T(8,128)S(1)} %get-tuple-element.52) | copy-start | bytes 393220
  80.0 10.7 %copy-start.4 = (f32[256,1024]{1,0:T(8,128)S(1)}, f32[256,1024]{1,0:T(8,128)}, u32[]{:S(2)}) copy-start(f32[256,1024]{1,0:T(8,128)} %get-tuple-element.18) | copy-start | bytes 3145732
  81.8 9.6 %copy-start.30 = (f32[1024]{0:T(1024)S(1)}, f32[1024]{0:T(1024)}, u32[]{:S(2)}) copy-start(f32[1024]{0:T(1024)} %param.25) | copy-start | bytes 12292
  85.6 18.7 %all-to-all-start.1 = ((bf16[4,256,512]{2,1,0:T(8,128)(2,1)}), bf16[4,256,512]{2,1,0:T(8,128)(2,1)}, u32[]{:S(2)}, u32[]{:S(2)}) async-start(bf16[4,256,512]{2,1,0:T(8,128)(2,1)} %broadcast_in_dim.70), calls=%async_computation.1 | async-start | bytes 2097152 | tf_op jit(solution)/shard_map/all_to_all | solution.py:19
  106.7 5.1 copy-start.37
  108.7 3.1 copy-start.38
  115.4 16.7 %copy-start.6 = (bf16[256,512]{1,0:T(8,128)(2,1)S(1)}, bf16[256,512]{1,0:T(8,128)(2,1)}, u32[]{:S(2)}) copy-start(bf16[256,512]{1,0:T(8,128)(2,1)} %param.14) | copy-start | bytes 786436
  115.5 26.6 %copy-start.32 = (f32[512]{0:T(512)S(1)}, f32[512]{0:T(512)}, u32[]{:S(2)}) copy-start(f32[512]{0:T(512)} %param.26) | copy-start | bytes 6148
  142.1 236.9 %copy-start.33 = (f32[256]{0:T(256)}, f32[256]{0:T(256)S(1)}, u32[]{:S(2)}) copy-start(f32[256]{0:T(256)S(1)} %add_rsqrt_fusion) | copy-start | bytes 3076
  144.3 21.2 %all-to-all-start.4 = ((bf16[4,256,512]{2,1,0:T(8,128)(2,1)}), bf16[4,256,512]{2,1,0:T(8,128)(2,1)}, u32[]{:S(2)}, u32[]{:S(2)}) async-start(bf16[4,256,512]{2,1,0:T(8,128)(2,1)} %broadcast_in_dim.73), calls=%async_computation.4 | async-start | bytes 2097152 | tf_op jit(solution)/shard_map/all_to_all | solution.py:19
  151.8 81.1 %reduce-scatter.7.cloned.1.call-start = ((), (), s32[]{:S(2)}) async-start(), calls=%async_computation.16 | async-start | bytes 7208960 | tf_op jit(solution)/shard_map/reduce_scatter | solution.py:138
  151.9 2.7 copy-start.13
  173.3 98.5 %reduce-scatter.11.cloned.1.call-start = ((), (), s32[]{:S(2)}) async-start(), calls=%async_computation.19 | async-start | bytes 3604480 | tf_op jit(solution)/shard_map/reduce_scatter | solution.py:138
  173.3 19.3 %copy-start.48 = (bf16[1408,512]{1,0:T(8,128)(2,1)S(1)}, bf16[1408,512]{1,0:T(8,128)(2,1)}, u32[]{:S(2)}) copy-start(bf16[1408,512]{1,0:T(8,128)(2,1)} %param.23) | copy-start | bytes 4325380
  196.0 142.0 %all-gather.8.cloned.1.call-start = ((), (), s32[]{:S(2)}) async-start(), calls=%async_computation.20 | async-start | bytes 7208960 | tf_op jit(solution)/shard_map/all_gather | solution.py:127
  276.8 90.1 %reduce-scatter.13.cloned.1.call-start = ((), (), s32[]{:S(2)}) async-start(), calls=%async_computation.21 | async-start | bytes 1310720 | tf_op jit(solution)/shard_map/reduce_scatter | solution.py:130
  345.7 85.0 %all-gather.6.cloned.1.call-start = ((), (), s32[]{:S(2)}) async-start(), calls=%async_computation.17 | async-start | bytes 3604480 | tf_op jit(solution)/shard_map/all_gather | solution.py:127
  385.4 18.2 %all-to-all-start.7 = ((bf16[4,256,512]{1,2,0:T(8,128)(2,1)}), bf16[4,256,512]{1,2,0:T(8,128)(2,1)}, u32[]{:S(2)}, u32[]{:S(2)}) async-start(bf16[4,256,512]{1,2,0:T(8,128)(2,1)} %broadcast_in_dim.76), calls=%async_computation.11 | async-start | bytes 2097152 | tf_op jit(solution)/shard_map/all_to_all | solution.py:19
  389.7 76.1 %all-reduce.10.cloned.1.call-start = ((), (), s32[]{:S(2)}) async-start(), calls=%async_computation.22 | async-start | bytes 2097152 | tf_op jit(solution)/shard_map/psum | solution.py:146
  410.2 4.3 copy-start.2
  415.5 2.3 copy-start.25
  420.6 51.8 %reduce-scatter.15.cloned.1.call-start = ((), (), s32[]{:S(2)}) async-start(), calls=%async_computation.23 | async-start | bytes 1310720 | tf_op jit(solution)/shard_map/reduce_scatter | solution.py:130
  420.6 3.0 copy-start.3
  420.7 3.1 copy-start.12
  425.9 80.8 %reduce-scatter.17.cloned.1.call-start = ((), (), s32[]{:S(2)}) async-start(), calls=%async_computation.24 | async-start | bytes 5242880 | tf_op jit(solution)/shard_map/reduce_scatter | solution.py:258
  430.7 5.2 copy-start.36
  430.7 154.6 %reduce-scatter.9.cloned.1.call-start = ((), (), s32[]{:S(2)}) async-start(), calls=%async_computation.18 | async-start | bytes 1310720 | tf_op jit(solution)/shard_map/reduce_scatter | solution.py:130
  435.8 199.8 %all-reduce.14.cloned.1.call-start = ((), (), s32[]{:S(2)}) async-start(), calls=%async_computation.26 | async-start | bytes 7340032 | tf_op jit(solution)/shard_map/psum | solution.py:325
  439.0 31.8 %copy-start.31 = (f32[512]{0:T(512)S(1)}, f32[512]{0:T(512)}, u32[]{:S(2)}) copy-start(f32[512]{0:T(512)} %param.24) | copy-start | bytes 6148
  470.9 20.7 %copy-start.17 = (f32[256,128]{1,0:T(8,128)S(1)}, f32[256,128]{1,0:T(8,128)}, u32[]{:S(2)}) copy-start(f32[256,128]{1,0:T(8,128)} %copy-done.16) | copy-start | bytes 393220
  494.0 274.9 %all-reduce.16.cloned.1.call-start = ((), (), s32[]{:S(2)}) async-start(), calls=%async_computation.27 | async-start | bytes 10747904 | tf_op jit(solution)/shard_map/psum | solution.py:333
  506.7 2.5 copy-start.10
  507.6 77.7 %copy-start.5 = (f32[256,512]{1,0:T(8,128)S(1)}, f32[256,512]{1,0:T(8,128)}, u32[]{:S(2)}) copy-start(f32[256,512]{1,0:T(8,128)} %get-tuple-element.31) | copy-start | bytes 1572868
  507.6 77.7 %copy-start.34 = (f32[256]{0:T(256)S(1)}, f32[256]{0:T(256)}, u32[]{:S(2)}) copy-start(f32[256]{0:T(256)} %copy-done.33) | copy-start | bytes 3076
  509.1 6.5 copy-start.44
  509.1 6.5 copy-start.46
  509.1 76.0 %copy-start.43 = (f32[256]{0:T(256)S(1)}, f32[256]{0:T(256)}, u32[]{:S(2)}) copy-start(f32[256]{0:T(256)} %copy-done.42) | copy-start | bytes 3076
  509.2 76.1 %copy-start.40 = (f32[256]{0:T(256)S(1)}, f32[256]{0:T(256)}, u32[]{:S(2)}) copy-start(f32[256]{0:T(256)} %copy-done.39) | copy-start | bytes 3076
  512.3 72.8 %all-to-all-start.8 = ((f32[4,1,256]{2,1,0:T(1,128)}), f32[4,1,256]{2,1,0:T(1,128)S(1)}, u32[]{:S(2)}, u32[]{:S(2)}) async-start(f32[4,1,256]{2,1,0:T(1,128)} %broadcast_in_dim.77), calls=%async_computation.13 | async-start | bytes 8192 | tf_op jit(solution)/shard_map/all_to_all | solution.py:19
  635.5 4.2 copy-start.18
  769.0 3.3 copy-start.15
  (18 other events, 21.5 us)
Sparse Core Ops, SparseCore 0:
  24.3 51.6 all-reduce.11
  173.4 59.4 reduce-scatter.6
  235.9 35.9 reduce-scatter.10
  277.0 61.0 all-gather.7
  348.5 38.0 all-gather.5
  420.7 44.9 all-reduce.9
Sparse Core Ops, SparseCore 1:
  26.3 48.0 all-gather.3
  345.8 21.1 reduce-scatter.12
  426.0 21.1 reduce-scatter.14
  450.3 46.0 reduce-scatter.16
  498.8 21.0 reduce-scatter.8
  524.6 110.9 all-reduce.13
  639.6 129.4 all-reduce.15
where the time goes:
time: 794 us; the launch traced here: 786 us
  waiting for transfers between devices  436 us (55%)
  blocking collectives  146 us (18%)
  matrix products  80.8 us (10%)
  other arithmetic  54.3 us (7%)
  local copies, waits for them, and re-layouts  31.3 us (4%)
  starting transfers between devices  20.9 us (3%)
  between operations  16.8 us (2%)
    psum x1, waiting for transfers between devices, shards(): lax.psum(grad_output.astype(jnp.bfloat16), 'dp').astype(jnp.float32)  127 us
    psum x2, waiting for transfers between devices, over_heads(): return lax.psum((first_part, second_part), 'row')  75.9 us
    reduce_scatter x2, waiting for transfers between devices, sum_to_rows(): lax.psum_scatter(term_fn(jnp.int32(0), row_share * lax.axis_size('row'))....  72.6 us
    psum x1, blocking collectives, shards(): lax.psum(grad_input_gain.astype(jnp.bfloat16), ('dp', 'col'))  67.8 us
    all_gather x2, waiting for transfers between devices, along_rows(): return lax.all_gather(values, 'row', axis=0, tiled=True)  61.2 us
    psum x1, waiting for transfers between devices, shards(): lax.psum(grad_latent_down.astype(jnp.bfloat16), ('dp', 'col'))  47.9 us
    all_to_all x4, blocking collectives, copy_for_each(): lax.all_to_all(jnp.broadcast_to(array[None], (size, *array.shape)), axis,...  42.3 us
    all_to_all x4, waiting for transfers between devices, copy_for_each(): lax.all_to_all(jnp.broadcast_to(array[None], (size, *array.shape)), axis,...  29.8 us
  transfers between devices with their start and end apart: 17, of which 11 were waited for; matrix products, arithmetic and copies ran while one was open for 15% of the time, Pallas kernels for 0%

commit v1 on v0

v1 whole, which is shorter than its diff:
```python
import math

import jax
import jax.numpy as jnp
from jax import lax
from jax.experimental import pallas as pl
from jax.experimental.pallas import tpu as pltpu
from jax.sharding import PartitionSpec as P

D = 2048
SEQ = 1024
PIECE = 256
epsilon = 1e-06
masked_value = -1e30
F32 = jnp.float32
BF = jnp.bfloat16
MESH = pl.DeviceIdType.MESH
VM = pl.BlockSpec(memory_space=pltpu.VMEM)
SM = pl.BlockSpec(memory_space=pltpu.SMEM)
ANY = pl.BlockSpec(memory_space=pl.ANY)
NN = (((1,), (0,)), ((), ()))
NT = (((1,), (1,)), ((), ()))
TN = (((0,), (0,)), ((), ()))


def dot(a, b, dims=NN):
    return lax.dot_general(a, b, dims, preferred_element_type=F32)


class Links:
    def __init__(self, ssem, rsem, lsem):
        self.ssem, self.rsem, self.lsem = ssem, rsem, lsem
        self.n, self.m, self.open = 0, 0, []

    def send(self, src, dst, dev):
        c = pltpu.make_async_remote_copy(
            src_ref=src, dst_ref=dst, send_sem=self.ssem.at[self.n], recv_sem=self.rsem.at[self.n],
            device_id=dev, device_id_type=MESH)
        self.n += 1
        c.start()
        self.open.append(c)
        return c

    def local(self, src, dst):
        c = pltpu.make_async_copy(src, dst, self.lsem.at[self.m])
        self.m += 1
        c.start()
        return c

    def close(self):
        for c in self.open:
            c.wait_send()


def place():
    r, c = lax.axis_index("row"), lax.axis_index("col")
    core = {"col": c + 1 - 2 * lax.rem(c, 2)}
    yl = {"col": lax.rem(c + 2, 4)}
    zs = [{"row": lax.rem(r + k, 4)} for k in (1, 2, 3)]
    return r, c, core, yl, zs


def x_peers():
    p = lax.axis_index("dp")
    x = lax.rem(p, 4)
    return x, [{"dp": p - x + lax.rem(x + k, 4)} for k in (1, 2, 3)]


def blk(c):
    return pl.ds(pl.multiple_of(c * 256, 256), 256)


class Gather16:
    def __init__(self, net, buf):
        r, c, core, yl, zs = place()
        self.net, self.buf, self.at = net, buf, (r, c, core, yl, zs)

    def put(self, a, b, dev):
        v = self.buf.at[a, blk(b)]
        return self.net.send(v, v, dev)

    def first(self):
        r, c, core, yl, zs = self.at
        self.y = self.put(r, c, yl)
        self.z2 = self.put(r, c, zs[1])
        self.zp = self.put(r, c, zs[0])
        self.zm = self.put(r, c, zs[2])
        self.cores = [self.put(r, c, core)]

    def second(self):
        r, c, core, yl, zs = self.at
        far = lax.rem(c + 2, 4)
        self.y.wait_recv()
        self.yp = self.put(r, far, zs[0])
        self.ym = self.put(r, far, zs[2])
        self.cores.append(self.put(r, far, core))
        self.z2.wait_recv()
        self.zy = self.put(lax.rem(r + 2, 4), c, yl)
        self.cores.append(self.put(lax.rem(r + 2, 4), c, core))
        self.zp.wait_recv()
        self.cores.append(self.put(lax.rem(r + 3, 4), c, core))
        self.zm.wait_recv()
        self.cores.append(self.put(lax.rem(r + 1, 4), c, core))

    def third(self):
        r, c, core, yl, zs = self.at
        far = lax.rem(c + 2, 4)
        self.yp.wait_recv()
        self.cores.append(self.put(lax.rem(r + 3, 4), far, core))
        self.ym.wait_recv()
        self.cores.append(self.put(lax.rem(r + 1, 4), far, core))
        self.zy.wait_recv()
        self.cores.append(self.put(lax.rem(r + 2, 4), far, core))

    def last(self):
        for h in self.cores:
            h.wait_recv()


class Scatter16:
    def __init__(self, net, part, ctx, crx, tx, rx):
        self.net, self.part, self.at = net, part, place()
        self.ctx, self.crx, self.tx, self.rx = ctx, crx, tx, rx

    def first(self):
        r, c, core, yl, zs = self.at
        other = c + 1 - 2 * lax.rem(c, 2)
        self.cores = []
        for slot in (5, 7, 6, 1, 3, 2, 4, 0):
            b = other if slot < 4 else lax.rem(other + 2, 4)
            self.ctx[slot] = self.part(slot % 4, b).astype(BF)
            self.cores.append((slot, self.net.send(self.ctx.at[slot], self.crx.at[slot], core)))
        self.cores = dict(self.cores)

    def mine(self, slot):
        r, c, core, yl, zs = self.at
        b = c if slot < 4 else lax.rem(c + 2, 4)
        own = self.part(slot % 4, b)
        self.cores[slot].wait_recv()
        return own + self.crx[slot].astype(F32)

    def go(self, i, value, dev):
        self.tx[i] = value.astype(BF)
        return self.net.send(self.tx.at[i], self.rx.at[i], dev)

    def take(self, i, h):
        h.wait_recv()
        return self.rx[i].astype(F32)

    def second(self):
        r, c, core, yl, zs = self.at
        self.bp = self.go(0, self.mine(5), zs[0])
        self.bm = self.go(1, self.mine(7), zs[2])
        self.a = self.go(2, self.mine(6), yl)
        self.cp = self.go(3, self.mine(1), zs[0])
        self.cm = self.go(4, self.mine(3), zs[2])

    def third(self):
        r, c, core, yl, zs = self.at
        t = self.mine(2)
        self.d = self.go(5, t + self.take(2, self.a), zs[1])
        t = self.mine(4)
        self.e = self.go(6, t + self.take(0, self.bp) + self.take(1, self.bm), yl)

    def last(self):
        t = self.mine(0)
        for i, h in ((3, self.cp), (4, self.cm), (5, self.d), (6, self.e)):
            t = t + self.take(i, h)
        return t


class Weights:
    def __init__(self, net, gate, up, down, gu, dn):
        self.net, self.gate, self.up, self.down, self.gu, self.dn = net, gate, up, down, gu, dn
        self.x, self.xs = x_peers()

    def own(self):
        r = lax.axis_index("row")
        lanes = pl.ds(pl.multiple_of(r * 384, 128), 384)
        self.locals = [
            self.net.local(self.gate.at[:, lanes], self.gu.at[0, :, pl.ds(0, 384)]),
            self.net.local(self.up.at[:, lanes], self.gu.at[0, :, pl.ds(384, 384)]),
            self.net.local(self.down.at[pl.ds(pl.multiple_of(r * 384, 128), 384)], self.dn.at[0])]

    def first(self):
        r, c, core, yl, zs = place()
        x, net = self.x, self.net
        rows = pl.ds(pl.multiple_of(x * 128, 128), 128)
        self.z = []
        for k in (2, 1, 3):
            d = lax.rem(r + k, 4)
            lanes = pl.ds(pl.multiple_of(d * 384, 128), 384)
            drows = pl.ds(pl.multiple_of(d * 384 + x * 96, 32), 96)
            slot = 4 - k
            self.z += [
                net.send(self.gate.at[rows, lanes], self.gu.at[slot, rows, pl.ds(0, 384)], zs[k - 1]),
                net.send(self.up.at[rows, lanes], self.gu.at[slot, rows, pl.ds(384, 384)], zs[k - 1]),
                net.send(self.down.at[drows], self.dn.at[slot, pl.ds(pl.multiple_of(x * 96, 32), 96)], zs[k - 1])]

    def second(self):
        x, net = self.x, self.net
        for h in self.z:
            h.wait_recv()
        g = self.gu.at[pl.ds(1, 3), pl.ds(pl.multiple_of(x * 128, 128), 128)]
        d = self.dn.at[pl.ds(1, 3), pl.ds(pl.multiple_of(x * 96, 32), 96)]
        self.h = []
        for k in (2, 1, 3):
            self.h += [net.send(g, g, self.xs[k - 1]), net.send(d, d, self.xs[k - 1])]

    def last(self):
        for h in self.h:
            h.wait_recv()
        for h in self.locals:
            h.wait()


def meet(peers):
    b = pltpu.get_barrier_semaphore()
    for p in peers:
        pl.semaphore_signal(b, inc=1, device_id=p, device_id_type=MESH)
    pl.semaphore_wait(b, len(peers))


def pack_stat(s, lanes=128):
    hi = s.astype(BF).astype(F32)
    lo = (s - hi).astype(BF).astype(F32)
    rest = s - hi - lo
    lane = lax.broadcasted_iota(jnp.int32, (s.shape[0], lanes), 1)
    return jnp.where(lane == 0, hi, jnp.where(lane == 1, lo, jnp.where(lane == 2, rest, 0.0))).astype(BF)


def unpack_stat(t):
    return jnp.sum(t.astype(F32), axis=1, keepdims=True)


def rope(u, cos, sin):
    a, b = u[:, :128], u[:, 128:]
    return jnp.concatenate([a * cos - b * sin, b * cos + a * sin], axis=1)


def unrope(g, cos, sin):
    a, b = g[:, :128], g[:, 128:]
    return jnp.concatenate([a * cos + b * sin, b * cos - a * sin], axis=1)


def attn_fwd_kernel(x_ref, docs_ref, starts_ref, ld_ref, kvw_ref, qu_hbm, ow_hbm, ig_ref, lg_ref, mg_ref,
                    cos_ref, sin_ref, cot_ref, gate_hbm, up_hbm, down_hbm,
                    ln_ref, lat_ref, rlat_ref, q_ref, kv_ref, w_ref, mix_ref, oall_ref, mid_ref, nm_ref, rmid_ref,
                    gu_ref, dn_ref, call_ref,
                    pf, ps, prx, qu_v, bias, bp, brx, st_tx, st_rx, ssem, rsem, lsem):
    r, c, core, yl, zs = place()
    net = Links(ssem, rsem, lsem)
    meet(zs + [core, yl] + x_peers()[1])
    ow_own = net.local(ow_hbm, oall_ref.at[c])
    ow_yl = net.send(ow_hbm, oall_ref.at[c], yl)
    ow_core = net.send(ow_hbm, oall_ref.at[c], core)
    qu_in = net.local(qu_hbm, qu_v)
    ffw = Weights(net, gate_hbm, up_hbm, down_hbm, gu_ref, dn_ref)
    ffw.own()
    call_ref[r, blk(c)] = cot_ref[...]
    cots = Gather16(net, call_ref)

    x = x_ref[...].astype(F32)
    xg = (x * ig_ref[...]).astype(BF)
    ssq = jnp.sum(x * x, axis=1, keepdims=True)
    pf[:, :1024] = dot(xg, ld_ref[...])
    pf[:, 1024:1536] = dot(xg, kvw_ref[...])
    pf[:, 1536:] = jnp.broadcast_to(ssq, (256, 128))
    stat = pack_stat(ssq)
    for d in range(4):
        rows = slice(64 * d, 64 * d + 64)
        ps[d, :, :1536] = pf[rows, :1536].astype(BF)
        ps[d, :, 1536:] = stat[rows]
    got = []
    for k in (2, 1, 3):
        got.append(net.send(ps.at[lax.rem(r + k, 4)], prx.at[k - 1], zs[k - 1]))

    qpos = c * 256 + lax.broadcasted_iota(jnp.int32, (256, SEQ), 0)
    kpos = lax.broadcasted_iota(jnp.int32, (256, SEQ), 1)
    number = lax.broadcasted_iota(jnp.int32, (8, SEQ), 0)
    onehot = (jnp.broadcast_to(docs_ref[...], (8, SEQ)) == number).astype(F32)
    onehot_q = (jnp.broadcast_to(docs_ref[:, pl.ds(pl.multiple_of(c * 256, 256), 256)], (8, 256))
                == number[:, :256]).astype(F32)
    same_doc = dot(onehot_q, onehot, TN) > 0.5
    ok = kpos <= qpos
    for m in range(2):
        s = starts_ref[0, m]
        ok = ok | ((qpos >= s) & (qpos < s + PIECE) & (kpos >= s) & (kpos < s + PIECE))
    bias[...] = jnp.where(same_doc & ok, 0.0, masked_value)

    own = pl.ds(pl.multiple_of(r * 64, 64), 64)
    for g in got:
        g.wait_recv()
    total = pf[own, :1536]
    ss = pf[own, 1536:1537]
    for k in range(3):
        total = total + prx[k, :, :1536].astype(F32)
        ss = ss + unpack_stat(prx[k, :, 1536:])
    r_in = lax.rsqrt(ss / D + epsilon)
    total = total * r_in
    cos64, sin64 = cos_ref[own, :], sin_ref[own, :]
    kv_rows = pl.ds(pl.multiple_of(c * 256 + r * 64, 64), 64)
    kv_ref[kv_rows, :256] = rope(total[:, 1024:1280], cos64, sin64).astype(BF)
    kv_ref[kv_rows, 256:] = total[:, 1280:1536].astype(BF)
    kv_got = [net.send(kv_ref.at[kv_rows], kv_ref.at[kv_rows], zs[k - 1]) for k in (2, 1, 3)]
    lat = total[:, :1024]
    r_lat = lax.rsqrt(jnp.mean(lat * lat, axis=1, keepdims=True) + epsilon)
    ln_ref[r, :, :1024] = (lat * r_lat * lg_ref[...]).astype(BF)
    ln_ref[r, :, 1024:] = pack_stat(r_in)
    ln_got = [net.send(ln_ref.at[r], ln_ref.at[r], zs[k - 1]) for k in (2, 1, 3)]
    lat_ref[...] = lat
    rlat_ref[...] = jnp.broadcast_to(r_lat, (64, 128))
    for g in kv_got:
        g.wait_recv()
    own_kv = kv_ref.at[pl.ds(pl.multiple_of(c * 256, 256), 256)]
    kv_yl = net.send(own_kv, own_kv, yl)
    kv_core = net.send(own_kv, own_kv, core)
    for g in ln_got:
        g.wait_recv()
    ffw.first()
    cots.first()
    qu_in.wait()
    cos, sin = cos_ref[...], sin_ref[...]
    ln_all = ln_ref[:, :, :1024].reshape(256, 1024)

    def make_query(h, carry):
        u = dot(ln_all, qu_v[:, pl.ds(pl.multiple_of(h * 256, 256), 256)])
        q_ref[h] = (rope(u, cos, sin) * (1.0 / 16.0)).astype(BF)
        return carry

    lax.fori_loop(0, 4, make_query, 0)
    kv_yl.wait_recv()
    far_kv = kv_ref.at[pl.ds(pl.multiple_of(lax.rem(c + 2, 4) * 256, 256), 256)]
    kv_far = net.send(far_kv, far_kv, core)
    ow_yl.wait_recv()
    ow_far = net.send(oall_ref.at[lax.rem(c + 2, 4)], oall_ref.at[lax.rem(c + 2, 4)], core)
    kv_core.wait_recv()
    kv_far.wait_recv()

    def head(h, carry):
        s = dot(q_ref[h], kv_ref[:, :256], NT) + bias[...]
        top = jnp.max(s, axis=1, keepdims=True)
        e = jnp.exp(s - top)
        w = (e / jnp.sum(e, axis=1, keepdims=True)).astype(BF)
        w_ref[h] = w
        mix_ref[:, pl.ds(pl.multiple_of(h * 256, 256), 256)] = dot(w, kv_ref[:, 256:]).astype(BF)
        return carry

    lax.fori_loop(0, 4, head, 0)
    ffw.second()
    cots.second()
    ow_own.wait()
    ow_core.wait_recv()
    ow_far.wait_recv()
    got = []
    for k in (2, 1, 3):
        d = lax.rem(r + k, 4)
        bp[k - 1] = dot(mix_ref[...], oall_ref[d]).astype(BF)
        got.append(net.send(bp.at[k - 1], brx.at[k - 1], zs[k - 1]))
    branch = dot(mix_ref[...], oall_ref[r])
    for g in got:
        g.wait_recv()
    for k in range(3):
        branch = branch + brx[k].astype(F32)
    middle = x_ref[...].astype(F32) + branch
    mid_ref[...] = middle
    ssm = jnp.sum(middle * middle, axis=1, keepdims=True)
    st_tx[...] = jnp.broadcast_to(ssm, (256, 128))
    got = [net.send(st_tx, st_rx.at[k - 1], zs[k - 1]) for k in (2, 1, 3)]
    for g in got:
        g.wait_recv()
    for k in range(3):
        ssm = ssm + st_rx[k, :, :1]
    r_mid = lax.rsqrt(ssm / D + epsilon)
    rmid_ref[...] = jnp.broadcast_to(r_mid, (256, 128))
    nm_ref[...] = (middle * r_mid * mg_ref[...]).astype(BF)
    cots.third()
    cots.last()
    ffw.last()
    net.close()


def S(shape, dtype=BF):
    return jax.ShapeDtypeStruct(shape, dtype)


def attn_fwd(x, docs, starts, ld, kvw, qu, ow, ig, lg, mg, cos, sin, cot, gate, up, down):
    return pl.pallas_call(
        attn_fwd_kernel,
        out_shape=(S((4, 64, 1152)), S((64, 1024), F32), S((64, 128), F32), S((4, 256, 256)), S((1024, 512)),
                   S((4, 256, 1024)), S((256, 1024)), S((4, 1024, 512)), S((256, 512), F32), S((256, 512)),
                   S((256, 128), F32), S((4, 512, 768)), S((4, 384, 512)), S((4, 1024, 512))),
        in_specs=[VM, VM, SM, VM, VM, ANY, ANY, VM, VM, VM, VM, VM, VM, ANY, ANY, ANY],
        out_specs=(VM,) * 14,
        scratch_shapes=[
            pltpu.VMEM((256, 1664), F32), pltpu.VMEM((4, 64, 1664), BF), pltpu.VMEM((3, 64, 1664), BF),
            pltpu.VMEM((1024, 1024), BF), pltpu.VMEM((256, 1024), F32), pltpu.VMEM((3, 256, 512), BF),
            pltpu.VMEM((3, 256, 512), BF), pltpu.VMEM((256, 128), F32), pltpu.VMEM((3, 256, 128), F32),
            pltpu.SemaphoreType.DMA((64,)), pltpu.SemaphoreType.DMA((64,)), pltpu.SemaphoreType.DMA((8,))],
        compiler_params=pltpu.CompilerParams(collective_id=0, has_side_effects=True, vmem_limit_bytes=56 << 20),
        name="attn_fwd",
    )(x, docs, starts, ld, kvw, qu, ow, ig, lg, mg, cos, sin, cot, gate, up, down)


def own_rope(local_rows):
    places = lax.axis_index("col") * local_rows + jnp.arange(local_rows, dtype=jnp.int32)
    freq = jnp.exp(-math.log(10000.0) * jnp.arange(128, dtype=F32) / 128)
    ang = places.astype(F32)[:, None] * freq[None, :]
    return jnp.cos(ang), jnp.sin(ang)


def ffn_kernel(nm_ref, gu_ref, dn_ref, call_ref, mid_ref, rmid_ref, mg_ref,
               out_ref, gmid_ref, gain_ref, ggu_out, gdn_out,
               m_ref, act_ref, gg_ref, ctx1, crx1, tx1, rx1, ctx2, crx2, tx2, rx2, st_tx, st_rx, ssem, rsem, lsem):
    r, c, core, yl, zs = place()
    net = Links(ssem, rsem, lsem)
    m_ref[r, blk(c)] = nm_ref[...]
    meet(zs + [core, yl])
    gather = Gather16(net, m_ref)
    gather.first()
    gather.second()
    gather.third()
    gather.last()

    def tile(t, carry):
        rows = blk(t)
        gu = jnp.zeros((256, 768), F32)
        ga = jnp.zeros((256, 384), F32)
        for k in range(4):
            f = lax.rem(r + k, 4)
            gu = gu + dot(m_ref[f, rows], gu_ref[k])
            ga = ga + dot(call_ref[f, rows], dn_ref[k], NT)
        g, u = gu[:, :384], gu[:, 384:]
        sig = 1.0 / (1.0 + jnp.exp(-g))
        silu = g * sig
        act_ref[rows] = (silu * u).astype(BF)
        gg_ref[rows, :384] = (ga * u * sig * (1.0 + g * (1.0 - sig))).astype(BF)
        gg_ref[rows, 384:] = (ga * silu).astype(BF)
        return carry

    lax.fori_loop(0, 4, tile, 0)
    back = Scatter16(net, lambda k, b: dot(gg_ref[blk(b)], gu_ref[k], NT), ctx1, crx1, tx1, rx1)
    back.first()
    back.second()

    def grads(k, carry):
        f = lax.rem(r + k, 4)
        ggu_out[f] = dot(m_ref[f], gg_ref[...], TN).astype(BF)
        gdn_out[f] = dot(act_ref[...], call_ref[f], TN).astype(BF)
        return carry

    lax.fori_loop(0, 2, grads, 0)
    back.third()
    lax.fori_loop(2, 4, grads, 0)
    fwd = Scatter16(net, lambda k, b: dot(act_ref[blk(b)], dn_ref[k]), ctx2, crx2, tx2, rx2)
    fwd.first()
    gm = back.last()
    middle, r_mid = mid_ref[...], rmid_ref[:, :1]
    gained = gm * mg_ref[...]
    stat = jnp.sum(gained * middle, axis=1, keepdims=True)
    st_tx[...] = jnp.broadcast_to(stat, (256, 128))
    got = [net.send(st_tx, st_rx.at[k - 1], zs[k - 1]) for k in (2, 1, 3)]
    gain_ref[...] = jnp.sum(gm * middle * r_mid, axis=0, keepdims=True)
    fwd.second()
    for g in got:
        g.wait_recv()
    for k in range(3):
        stat = stat + st_rx[k, :, :1]
    gmid_ref[...] = call_ref[r, blk(c)].astype(F32) + r_mid * gained - middle * (r_mid * r_mid * r_mid * stat / D)
    fwd.third()
    out_ref[...] = (middle + fwd.last()).astype(BF)
    net.close()


def ffn(nm, gu, dn, call, mid, rmid, mg):
    big = [pltpu.VMEM((8, 256, 512), BF), pltpu.VMEM((8, 256, 512), BF), pltpu.VMEM((7, 256, 512), BF),
           pltpu.VMEM((7, 256, 512), BF)]
    return pl.pallas_call(
        ffn_kernel,
        out_shape=(S((256, 512)), S((256, 512), F32), S((1, 512), F32), S((4, 512, 768)), S((4, 384, 512))),
        in_specs=[VM] * 7,
        out_specs=(VM,) * 5,
        scratch_shapes=[pltpu.VMEM((4, 1024, 512), BF), pltpu.VMEM((1024, 384), BF), pltpu.VMEM((1024, 768), BF),
                        *big, *big, pltpu.VMEM((256, 128), F32), pltpu.VMEM((3, 256, 128), F32),
                        pltpu.SemaphoreType.DMA((64,)), pltpu.SemaphoreType.DMA((64,)),
                        pltpu.SemaphoreType.DMA((1,))],
        compiler_params=pltpu.CompilerParams(collective_id=1, has_side_effects=True, vmem_limit_bytes=58 << 20),
        name="ffn",
    )(nm, gu, dn, call, mid, rmid, mg)


def shards(tokens, documents, piece_starts, latent_down, key_value, query_up, output_weight, gate_weight, up_weight,
           down_weight, input_gain, latent_gain, middle_gain, cotangent):
    cos, sin = own_rope(256)
    lnst, lat, rlat, q, kv, w, mix, oall, mid, nm, rmid, gu, dn, call = attn_fwd(
        tokens, documents, piece_starts, latent_down, key_value, query_up, output_weight, input_gain[None],
        latent_gain[None], middle_gain[None], cos, sin, cotangent, jnp.pad(gate_weight, ((0, 0), (0, 128))),
        jnp.pad(up_weight, ((0, 0), (0, 128))), jnp.pad(down_weight, ((0, 128), (0, 0))))
    out, gmid, gain_mid, ggu, gdn = ffn(nm, gu, dn, call, mid, rmid, middle_gain[None])
    a = lax.psum_scatter(ggu.reshape(4, 8, 64, 768), "dp", scatter_dimension=1)
    b = lax.psum_scatter(gdn.reshape(4, 8, 48, 512), "dp", scatter_dimension=1)
    a = lax.all_to_all(a, "row", 0, 0, tiled=True)
    b = lax.all_to_all(b, "row", 0, 0, tiled=True)
    a = jnp.moveaxis(a, 0, 1)
    a = lax.all_gather(a, "dp", axis=0, tiled=True)
    b = lax.all_gather(b, "dp", axis=1)
    grad_gate = a[:, :, :384].reshape(512, 1536)[:, :1408].astype(F32)
    grad_up = a[:, :, 384:].reshape(512, 1536)[:, :1408].astype(F32)
    grad_down = b.reshape(1536, 512)[:1408].astype(F32)
    r, c = lax.axis_index("row"), lax.axis_index("col")
    gb = gmid.astype(BF)
    gb_all = lax.all_gather(gb, "row", axis=0)
    gmix = sum(jnp.dot(gb_all[k], oall[k].T, preferred_element_type=F32) for k in range(4)).astype(BF)
    gout = jnp.einsum("tm,ktn->mkn", mix, gb_all, preferred_element_type=F32).reshape(1024, 2048)
    gout = lax.psum_scatter(gout.astype(BF), "col", scatter_dimension=1, tiled=True)
    gout = lax.psum(gout, "dp").astype(F32)
    gmix = gmix.reshape(256, 4, 256)
    keys, values = kv[:, :256], kv[:, 256:]
    gw = jnp.einsum("qhd,kd->hqk", gmix, values, preferred_element_type=F32)
    wf = w.astype(F32)
    gs = (wf * (gw - jnp.sum(gw * wf, axis=2, keepdims=True))).astype(BF)
    gq = jnp.einsum("hqk,kd->qhd", gs, keys, preferred_element_type=F32) / 16.0
    gk = jnp.einsum("hqk,hqd->kd", gs, q, preferred_element_type=F32)
    gv = jnp.einsum("hqk,qhd->kd", w, gmix, preferred_element_type=F32)

    def un(g, cs, sn):
        a, b = g[..., :128], g[..., 128:]
        return jnp.concatenate([a * cs + b * sn, b * cs - a * sn], axis=-1)

    gqr = un(gq, cos[:, None], sin[:, None]).reshape(256, 1024).astype(BF)
    ln = lnst[:, :, :1024].reshape(256, 1024)
    r_in = jnp.sum(lnst[:, :, 1024:1027].astype(F32), axis=2).reshape(256, 1)
    gqu = jnp.dot(ln.T, gqr, preferred_element_type=F32)
    gln = lax.psum_scatter(jnp.dot(gqr, query_up.T, preferred_element_type=F32).astype(BF), "row",
                           scatter_dimension=0, tiled=True).astype(F32)
    gkv = lax.psum_scatter(jnp.concatenate([gk, gv], axis=1).astype(BF), ("col", "row"),
                           scatter_dimension=0, tiled=True).astype(F32)
    cs, sn = lax.dynamic_slice_in_dim(cos, r * 64, 64, 0), lax.dynamic_slice_in_dim(sin, r * 64, 64, 0)
    rl = rlat[:, :1]
    gained = gln * latent_gain
    glat = rl * gained - lat * (rl**3 * jnp.mean(gained * lat, axis=1, keepdims=True))
    glg = jnp.sum(gln * lat * rl, axis=0)
    glat = jnp.concatenate([glat, un(gkv[:, :256], cs, sn), gkv[:, 256:]], axis=1).astype(BF)
    glat = lax.all_gather(glat, "row", axis=0, tiled=True)
    x = tokens.astype(F32)
    normed = (x * r_in * input_gain).astype(BF)
    gld = jnp.dot(normed.T, glat, preferred_element_type=F32)
    gn = jnp.dot(glat[:, :1024], latent_down.T, preferred_element_type=F32)
    gn = gn + jnp.dot(glat[:, 1024:], key_value.T, preferred_element_type=F32)
    gained = gn * input_gain
    stat = lax.psum(jnp.sum(gained * x, axis=1, keepdims=True), "row")
    gx = gmid + r_in * gained - x * (r_in**3 * stat / D)
    gig = jnp.sum(gn * x * r_in, axis=0)
    gld, gqu = lax.psum((gld.astype(BF), gqu.astype(BF)), ("dp", "col"))
    gig, gmg = lax.psum((gig, gain_mid[0]), ("dp", "col"))
    glg = lax.psum(glg, ("dp", "row", "col"))
    return (out, gx.astype(BF), gld[:, :1024].astype(F32), gld[:, 1024:].astype(F32), gqu.astype(F32), gout,
            grad_gate, grad_up, grad_down, gig, glg, gmg)


def solution(mesh):
    placed = (P(("dp", "col"), "row"), P("dp", None), P("dp", None), P("row", None), P("row", None), P(None, "row"),
              P("row", "col"), P("row", "col"), P("row", "col"), P("col", "row"), P("row"), P(), P("row"),
              P(("dp", "col"), "row"))
    return jax.shard_map(
        shards, mesh=mesh, in_specs=placed,
        out_specs=(P(("dp", "col"), "row"), P(("dp", "col"), "row"), P("row", None), P("row", None), P(None, "row"),
                   P("row", "col"), P("row", "col"), P("row", "col"), P("col", "row"), P("row"), P(), P("row")),
        check_vma=False)
```

time: 794 us -> 761 us (0.958)
  Pallas kernels: 0 us -> 180 us
  waiting for transfers between devices: 436 us -> 311 us
  matrix products: 80.8 us -> 20.4 us
  other arithmetic: 54.3 us -> 24.4 us
  blocking collectives: 146 us -> 167 us
  starting transfers between devices: 20.9 us -> 0.59 us
  local copies, waits for them, and re-layouts: 31.3 us -> 41.8 us
    pallas_call x0 -> x2, Pallas kernels: none -> 180 us  [the longest x1 94.8 us: attn_fwd(): pl.pallas_call(attn_fwd_kernel, out_shape=(S((4, 64, 1152)), S((64, 1024)...]
    psum x4 -> x2, waiting for transfers between devices: 250 us -> 124 us  [the longest x1 124 us: shards(): gout = lax.psum(gout, 'dp').astype(F32)]
    dot_general x23 -> x14, matrix products: 79.8 us -> 20.4 us  [the longest x4 5.26 us: shards(): jnp.dot(gb_all[k], oall[k].T, preferred_element_type=F32)]
    psum x2 -> x3, blocking collectives: 86.8 us -> 137 us  [the longest x1 65.1 us: shards(): glg = lax.psum(glg, ('dp', 'row', 'col'))]
    all_to_all x5 -> x2, blocking collectives: 58.8 us -> 17.8 us  [the longest x1 9.22 us: shards(): b = lax.all_to_all(b, 'row', 0, 0, tiled=True)]
    all_to_all x4 -> x0, waiting for transfers between devices: 29.8 us -> none  [copy_for_each(): lax.all_to_all(jnp.broadcast_to(array[None], (size, *array.shape)), axis,...]
    all_to_all x4 -> x0, starting transfers between devices: 20 us -> none  [copy_for_each(): lax.all_to_all(jnp.broadcast_to(array[None], (size, *array.shape)), axis,...]
    all_gather x3, waiting for transfers between devices: 61.2 us -> 77.7 us  [the longest x1 56.1 us: shards(): a = lax.all_gather(a, 'dp', axis=0, tiled=True)]
  transfers between devices with their start and end apart: 17 -> 8, of which waited for: 11 -> 6; matrix products, arithmetic and copies ran while one was open for 15% -> 6% of each run, Pallas kernels for 0% -> 0%
where the time goes in v1:
time: 761 us; the launch traced here: 759 us
  waiting for transfers between devices  311 us (41%)
  Pallas kernels  180 us (24%)
  blocking collectives  167 us (22%)
  local copies, waits for them, and re-layouts  41.8 us (5%)
  other arithmetic  24.4 us (3%)
  matrix products  20.4 us (3%)
  between operations  14.5 us (2%)
    psum x1, waiting for transfers between devices, shards(): gout = lax.psum(gout, 'dp').astype(F32)  124 us
    pallas_call x1, Pallas kernels, attn_fwd(): pl.pallas_call(attn_fwd_kernel, out_shape=(S((4, 64, 1152)), S((64, 1024)...  94.8 us
    pallas_call x1, Pallas kernels, ffn(): pl.pallas_call(ffn_kernel, out_shape=(S((256, 512)), S((256, 512), F32),...  84.9 us
    psum x1, blocking collectives, shards(): glg = lax.psum(glg, ('dp', 'row', 'col'))  65.1 us
    psum x1, blocking collectives, shards(): gig, gmg = lax.psum((gig, gain_mid[0]), ('dp', 'col'))  64.6 us
    reduce_scatter x1, waiting for transfers between devices, shards(): lax.psum_scatter(jnp.concatenate([gk, gv], axis=1).astype(BF), ('col', 'r...  61.6 us
    all_gather x1, waiting for transfers between devices, shards(): a = lax.all_gather(a, 'dp', axis=0, tiled=True)  56.1 us
    reduce_scatter x1, waiting for transfers between devices, shards(): lax.psum_scatter(gout.astype(BF), 'col', scatter_dimension=1, tiled=True)  27.6 us
  transfers between devices with their start and end apart: 8, of which 6 were waited for; matrix products, arithmetic and copies ran while one was open for 6% of the time, Pallas kernels for 0%

profile of v1, /device:TPU:1, one launch (start us, length us, event | category | flops | bytes accessed | tf_op | source)
XLA Modules:
  0.0 759.5 jit_solution(12401808789164890863)
XLA Ops:
  7.3 2.7 pad.11.gate_hbm
  10.0 1.3 pad.12.up_hbm
  11.9 1.2 pad.13.down_hbm
  13.2 1.2 multiply_sine_fusion
  14.4 94.8 %attn_fwd.1 = (bf16[4,64,1152]{2,1,0:T(8,128)(2,1)}, f32[64,1024]{1,0:T(8,128)}, f32[64,128]{1,0:T(8,128)}, bf16[4,256,256]{2,1,0:T(8,128)(2,1)}, bf16[1024,512]...) custom-call(bf16[256,512]{1,0:T(8,128)(2,1)} %x_ref.1, ...), custom_call_target="tpu_custom_call" | custom-call | tf_op jit(solution)/shard_map/attn_fwd/pallas_call | solution.py:388
  109.3 84.9 %ffn.1 = (bf16[256,512]{1,0:T(8,128)(2,1)}, f32[256,512]{1,0:T(8,128)}, f32[1,512]{1,0:T(1,128)}, bf16[4,512,768]{2,1,0:T(8,128)(2,1)}, bf16[4,384,512]{2,1,0:T(8,128)(2,1)}) custom-call(bf16[256,512]{1,0:T(8,128)(2,1)} %get-tuple-element.31.nm_ref, bf16[4,512,768]{2,1,0:T(8,128)(2,1)} %get-tuple-element.32.gu_ref, ...), custom_call_target="tpu_custom_call" | custom-call | tf_op jit(solution)/shard_map/ffn/pallas_call | solution.py:478
  194.2 1.8 convert_element_type.96
  196.0 21.6 %all-gather.8.cloned.1.call-done = bf16[1024,512]{1,0:T(8,128)(2,1)} async-done(((bf16[256,512]{1,0:T(8,128)(2,1)}), bf16[1024,512]{1,0:T(8,128)(2,1)}) %all-gather.8.cloned.1.call-update) | async-done | bytes 1048592 | tf_op jit(solution)/shard_map/all_gather | solution.py:512
  217.6 4.5 convolution_convert_fusion.1
  222.2 6.6 copy.109
  230.5 1.8 fusion.9
  232.3 1.7 convolution_add_fusion.2
  234.5 1.3 fusion.3
  235.8 1.2 copy.130
  237.1 1.9 fusion
  241.7 1.3 copy-done.8
  243.0 1.6 convolution_convert_fusion.3
  247.1 1.1 pad_maximum_fusion
  248.3 27.6 %reduce-scatter.14.cloned.1.call-done = bf16[1024,512]{1,0:T(8,128)(2,1)} async-done(((bf16[1024,2048]{1,0:T(8,128)(2,1)}), bf16[1024,512]{1,0:T(8,128)(2,1)}) %reduce-scatter.14.cloned.1.call-update) | async-done | bytes 1048592 | tf_op jit(solution)/shard_map/reduce_scatter | solution.py:515
  277.3 2.1 convolution_convert_fusion.2
  279.4 20.2 %reduce-scatter.10.cloned.1.call-done = bf16[64,1024]{1,0:T(8,128)(2,1)} async-done(((bf16[256,1024]{1,0:T(8,128)(2,1)}), bf16[64,1024]{1,0:T(8,128)(2,1)}) %reduce-scatter.10.cloned.1.call-update) | async-done | bytes 131088 | tf_op jit(solution)/shard_map/reduce_scatter | solution.py:534
  299.6 1.1 fusion.35
  301.0 1.0 fusion.32
  302.0 61.6 %reduce-scatter.12.cloned.1.call-done = bf16[64,512]{1,0:T(8,128)(2,1)} async-done(((bf16[1024,512]{1,0:T(8,128)(2,1)}), bf16[64,512]{1,0:T(8,128)(2,1)}) %reduce-scatter.12.cloned.1.call-update) | async-done | bytes 65552 | tf_op jit(solution)/shard_map/reduce_scatter | solution.py:536
  365.3 11.8 %all_gather.20 = bf16[256,1536]{1,0:T(8,128)(2,1)S(1)} all-gather(bf16[64,1536]{1,0:T(8,128)(2,1)S(1)} %pad_maximum_fusion.1), channel_id=1, replica_groups=mesh['dp'=8,'row'=4,'col'=4] {'row'}, dimensions={0}, use_global_device_ids=true | all-gather | bytes 983040 | tf_op jit(solution)/shard_map/all_gather | solution.py:544
  377.1 1.8 convolution_convert_fusion
  380.2 123.7 %all-reduce.13.cloned.1.call-done = (bf16[1024,512]{1,0:T(8,128)(2,1)}, bf16[4,8,64,768]{3,2,1,0:T(8,128)(2,1)}, bf16[4,8,48,512]{3,2,1,0:T(8,128)(2,1)}) async-done(((bf16[1024,512]{1,0:T(8,128)(2,1)}, bf16[4,8,64,768]{3,2,1,0:T(8,128)(2,1)}, bf16[4,8,48,512]{3,2,1,0:T(8,128)(2,1)}), (bf16[1024,512]{1,0:T(8,128)(2,1)}, bf16[4,8,64,768]{3,2,1,0:T(8,128)(2,1)}, ...) | async-done | bytes 5767184 | tf_op jit(solution)/shard_map/psum | solution.py:516
  503.9 1.6 dynamic-slice_bitcast_fusion.1
  505.5 9.2 %all_to_all.10 = bf16[4,48,512]{2,1,0:T(8,128)(2,1)} all-to-all(bf16[4,48,512]{2,1,0:T(8,128)(2,1)S(1)} %dynamic-slice_bitcast_fusion.1), channel_id=1, replica_groups=mesh['dp'=8,'row'=4,'col'=4] {'row'}, dimensions={0} | all-to-all | bytes 393216 | tf_op jit(solution)/shard_map/all_to_all | solution.py:503
  514.8 1.7 dynamic-slice_bitcast_fusion
  516.5 8.6 %all_to_all.11 = bf16[4,64,768]{2,1,0:T(8,128)(2,1)S(1)} all-to-all(bf16[4,64,768]{2,1,0:T(8,128)(2,1)S(1)} %dynamic-slice_bitcast_fusion), channel_id=1, replica_groups=mesh['dp'=8,'row'=4,'col'=4] {'row'}, dimensions={0} | all-to-all | bytes 786432 | tf_op jit(solution)/shard_map/all_to_all | solution.py:502
  525.2 1.1 copy.110
  526.3 65.1 %psum.54 = f32[1024]{0:T(1024)} all-reduce(f32[1024]{0:T(1024)S(1)} %get-tuple-element.88), channel_id=1, replica_groups=mesh['dp'=8,'row'=4,'col'=4] {'dp','row','col'}, use_global_device_ids=true, to_apply=%region_16.17 | all-reduce | flops 1024 | bytes 8192 | tf_op jit(solution)/shard_map/psum | solution.py:556
  592.4 7.7 %psum.49 = f32[256,1]{0,1:T(1,128)S(1)} all-reduce(f32[256,1]{0,1:T(1,128)S(1)} %bitcast.107), channel_id=1, replica_groups=mesh['dp'=8,'row'=4,'col'=4] {'row'}, use_global_device_ids=true, to_apply=%region_6.7 | all-reduce | flops 256 | bytes 2048 | tf_op jit(solution)/shard_map/psum | solution.py:551
  600.1 64.6 %all-reduce.5 = (f32[512]{0:T(512)}, f32[512]{0:T(512)}) all-reduce(f32[512]{0:T(512)S(1)} %get-tuple-element.86, f32[512]{0:T(512)S(1)} %bitcast.106), channel_id=1, replica_groups=mesh['dp'=8,'row'=4,'col'=4] {'dp','col'}, use_global_device_ids=true, to_apply=%region_14.15 | all-reduce | flops 1024 | bytes 8192 | tf_op jit(solution)/shard_map/psum | solution.py:555
  665.6 4.2 convert_element_type.111
  669.8 1.1 slice_convert_fusion.4
  670.9 1.6 slice_convert_fusion.3
  672.5 1.6 convert_element_type.114
  674.1 3.3 slice_convert_fusion
  677.5 56.1 %all-gather.6.cloned.1.call-done = bf16[512,4,768]{2,1,0:T(4,128)(2,1)} async-done(((bf16[64,4,768]{2,1,0:T(4,128)(2,1)}), bf16[512,4,768]{2,1,0:T(4,128)(2,1)}) %all-gather.6.cloned.1.call-update) | async-done | bytes 3145744 | tf_op jit(solution)/shard_map/all_gather | solution.py:505
  733.5 4.1 fusion.49
  737.6 2.5 copy.128
  740.2 1.8 slice_convert_fusion.2
  741.9 2.2 copy.113
  744.2 3.8 copy.129
  748.0 1.8 slice_convert_fusion.1
  749.7 2.2 copy.114
  (102 shorter events, 15.5 us)
Async XLA Ops:
  7.2 2.8 copy-start.10
  7.2 210.4 %all-gather.8.cloned.1.call-start = ((), (), s32[]{:S(2)}) async-start(), calls=%async_computation.9 | async-start | bytes 1310720 | tf_op jit(solution)/shard_map/all_gather | solution.py:512
  10.0 1.9 copy-start.11
  109.2 108.4 %copy-start.20 = (bf16[256,1024]{1,0:T(8,128)(2,1)S(1)}, bf16[256,1024]{1,0:T(8,128)(2,1)}, u32[]{:S(2)}) copy-start(bf16[256,1024]{1,0:T(8,128)(2,1)} %get-tuple-element.46) | copy-start | bytes 1572868
  196.0 79.9 %reduce-scatter.14.cloned.1.call-start = ((), (), s32[]{:S(2)}) async-start(), calls=%async_computation.7 | async-start | bytes 5242880 | tf_op jit(solution)/shard_map/reduce_scatter | solution.py:515
  228.7 0.9 copy-start.13
  228.7 1.0 copy-start.12
  228.7 1.8 copy-start.4
  228.8 70.9 %reduce-scatter.10.cloned.1.call-start = ((), (), s32[]{:S(2)}) async-start(), calls=%async_computation.5 | async-start | bytes 655360 | tf_op jit(solution)/shard_map/reduce_scatter | solution.py:534
  230.5 3.5 copy-start.3
  234.5 2.5 copy-start
  239.0 1.4 copy-start.15
  240.4 1.3 copy-start.1
  240.4 1.0 copy-start.19
  241.4 1.6 copy-start.8
  244.6 119.0 %reduce-scatter.12.cloned.1.call-start = ((), (), s32[]{:S(2)}) async-start(), calls=%async_computation.6 | async-start | bytes 1114112 | tf_op jit(solution)/shard_map/reduce_scatter | solution.py:536
  244.6 1.7 copy-start.2
  244.6 1.7 copy-start.26
  248.2 255.7 %all-reduce.13.cloned.1.call-start = ((), (), s32[]{:S(2)}) async-start(), calls=%async_computation.12 | async-start | bytes 11534336 | tf_op jit(solution)/shard_map/psum | solution.py:516
  275.8 1.1 copy-start.18
  275.8 1.3 copy-start.22
  275.9 389.8 %all-reduce.11.cloned.1.call-start = ((), (), s32[]{:S(2)}) async-start(), calls=%async_computation.11 | async-start | bytes 7340032 | tf_op jit(solution)/shard_map/psum | solution.py:554
  276.9 22.7 %copy-start.16 = (f32[64,1024]{1,0:T(8,128)S(1)}, f32[64,1024]{1,0:T(8,128)}, u32[]{:S(2)}) copy-start(f32[64,1024]{1,0:T(8,128)} %get-tuple-element.44) | copy-start | bytes 786436
  276.9 22.7 %copy-start.23 = (f32[1024]{0:T(1024)S(1)}, f32[1024]{0:T(1024)}, u32[]{:S(2)}) copy-start(f32[1024]{0:T(1024)} %param.25) | copy-start | bytes 12292
  279.4 97.7 %copy-start.5 = (bf16[256,512]{1,0:T(8,128)(2,1)S(1)}, bf16[256,512]{1,0:T(8,128)(2,1)}, u32[]{:S(2)}) copy-start(bf16[256,512]{1,0:T(8,128)(2,1)} %x_ref.1) | copy-start | bytes 786436
  279.4 97.7 %copy-start.24 = (f32[512]{0:T(512)S(1)}, f32[512]{0:T(512)}, u32[]{:S(2)}) copy-start(f32[512]{0:T(512)} %param.24) | copy-start | bytes 6148
  378.9 0.7 copy-start.27
  379.0 212.5 %copy-start.6 = (bf16[512,512]{1,0:T(8,128)(2,1)S(1)}, bf16[512,512]{1,0:T(8,128)(2,1)}, u32[]{:S(2)}) copy-start(bf16[512,512]{1,0:T(8,128)(2,1)} %kvw_ref.1) | copy-start | bytes 1572868
  379.0 295.1 %all-gather.10.cloned.1.call-start = ((), (), s32[]{:S(2)}) async-start(), calls=%async_computation.10 | async-start | bytes 1769472 | tf_op jit(solution)/shard_map/all_gather | solution.py:506
  514.7 77.1 %copy-start.17 = (bf16[512,1024]{1,0:T(8,128)(2,1)S(1)}, bf16[512,1024]{1,0:T(8,128)(2,1)}, u32[]{:S(2)}) copy-start(bf16[512,1024]{1,0:T(8,128)(2,1)} %ld_ref.1) | copy-start | bytes 3145732
  514.7 218.8 %all-gather.6.cloned.1.call-start = ((), (), s32[]{:S(2)}) async-start(), calls=%async_computation.8 | async-start | bytes 3538944 | tf_op jit(solution)/shard_map/all_gather | solution.py:505
  591.4 8.7 %copy-start.25 = (f32[1,512]{1,0:T(1,128)S(1)}, f32[1,512]{1,0:T(1,128)}, u32[]{:S(2)}) copy-start(f32[1,512]{1,0:T(1,128)} %get-tuple-element.49) | copy-start | bytes 6148
  591.4 73.3 %copy-start.7 = (f32[256,512]{1,0:T(8,128)S(1)}, f32[256,512]{1,0:T(8,128)}, u32[]{:S(2)}) copy-start(f32[256,512]{1,0:T(8,128)} %get-tuple-element.38) | copy-start | bytes 1572868
  665.6 4.2 copy-start.9
  669.8 2.7 copy-start.14
  749.7 2.2 copy-start.21
Sparse Core Ops, SparseCore 0:
  196.1 21.4 all-gather.7
  228.9 46.9 reduce-scatter.13
  278.9 20.6 reduce-scatter.9
  302.5 61.0 reduce-scatter.11
  366.2 137.6 all-reduce.12
  507.8 107.8 all-reduce.10
  617.9 49.5 all-gather.9
  670.4 63.0 all-gather.5

commit v2 on v1

--- a/solution.py
+++ b/solution.py
@@ -489,73 +489,368 @@
     )(nm, gu, dn, call, mid, rmid, mg)
 
 
+def rows_of(start, n):
+    return pl.ds(pl.multiple_of(start, n & -n), n)
+
+
+def ring_scatter(net, src, tx, rx, x, xs):
+    f = lambda v: v[...].astype(F32)
+    n1, n2, n3 = (lax.rem(x + k, 4) for k in (1, 2, 3))
+    m1 = net.send(src(n2, 0), rx.at[0], xs[0])
+    m2 = net.send(src(n2, 1), rx.at[1], xs[2])
+    m3 = net.send(src(n1, 1), rx.at[2], xs[0])
+    m4 = net.send(src(n3, 0), rx.at[3], xs[2])
+    yield
+    m1.wait_recv()
+    tx[0] = (f(src(n1, 0)) + f(rx.at[0])).astype(BF)
+    m5 = net.send(tx.at[0], rx.at[4], xs[0])
+    m2.wait_recv()
+    tx[1] = (f(src(n3, 1)) + f(rx.at[1])).astype(BF)
+    m6 = net.send(tx.at[1], rx.at[5], xs[2])
+    yield
+    m3.wait_recv()
+    m4.wait_recv()
+    m5.wait_recv()
+    m6.wait_recv()
+    return f(src(x, 0)) + f(rx.at[3]) + f(rx.at[4]), f(src(x, 1)) + f(rx.at[2]) + f(rx.at[5])
+
+
+def ring_gather(net, view, x, xs):
+    n1, n3 = lax.rem(x + 1, 4), lax.rem(x + 3, 4)
+    p = net.send(view(x, None), view(x, None), xs[0])
+    m = net.send(view(x, None), view(x, None), xs[2])
+    yield
+    p.wait_recv()
+    p = net.send(view(n3, 0), view(n3, 0), xs[0])
+    m.wait_recv()
+    m = net.send(view(n1, 1), view(n1, 1), xs[2])
+    yield
+    p.wait_recv()
+    m.wait_recv()
+
+
+def pair_scatter(net, both, rx, bit, dev):
+    h = net.send(both.at[1 - bit], rx, dev)
+    yield
+    h.wait_recv()
+    return both[bit].astype(F32) + rx[...].astype(F32)
+
+
+def pair_gather(net, view, dev):
+    h = net.send(view, view, dev)
+    yield
+    h.wait_recv()
+
+
+def reduce_dp(net, at, src, buf, fin, n, spread):
+    x, xs, yh, yhd = at
+    tx, rx, both, prx = buf
+    a, b = yield from ring_scatter(net, src, tx, rx, x, xs)
+    both[0] = a.astype(BF)
+    both[1] = b.astype(BF)
+    t = yield from pair_scatter(net, both, prx, yh, yhd)
+    piece = rows_of(x * 2 * n + yh * n, n)
+    yield from spread(t, piece)
+    yield from pair_gather(net, fin(piece), yhd)
+
+    def view(j, h):
+        return fin(rows_of(j * 2 * n, 2 * n) if h is None else rows_of(j * 2 * n + h * n, n))
+
+    yield from ring_gather(net, view, x, xs)
+
+
+def reduce_all(net, at, part, buf, fin):
+    x, xs, yh, yhd, core, coredev, yl, yldev = at
+    crx, csum, tx, rx, both, yrx, both2, prx = buf
+    half = part.shape[0] // 2
+    n = half // 8
+    h = net.send(part.at[rows_of((1 - core) * half, half)], crx, coredev)
+    yield
+    h.wait_recv()
+    csum[...] = (part[rows_of(core * half, half)].astype(F32) + crx[...].astype(F32)).astype(BF)
+    a, b = yield from ring_scatter(net, lambda j, h: csum.at[rows_of(j * 2 * n + h * n, n)], tx, rx, x, xs)
+    both[0] = a.astype(BF)
+    both[1] = b.astype(BF)
+    t = yield from pair_scatter(net, both, yrx, yl, yldev)
+    both2[0] = t[:n // 2].astype(BF)
+    both2[1] = t[n // 2:].astype(BF)
+    t = yield from pair_scatter(net, both2, prx, yh, yhd)
+    base = core * half + x * 2 * n + yl * n
+    fin[rows_of(base + yh * (n // 2), n // 2)] = t.astype(BF)
+    v = fin.at[rows_of(base + yh * (n // 2), n // 2)]
+    yield from pair_gather(net, v, yhd)
+    yield from pair_gather(net, fin.at[rows_of(base, n)], yldev)
+
+    def view(j, h):
+        s = core * half + j * 2 * n
+        return fin.at[rows_of(s, 2 * n)] if h is None else fin.at[rows_of(s + h * n, n)]
+
+    yield from ring_gather(net, view, x, xs)
+    yield from pair_gather(net, fin.at[rows_of(core * half, half)], coredev)
+
+
+def reduce_vec(net, at, zs, v, rx):
+    x, xs, yh, yhd, core, coredev, yl, yldev = at
+    hs = [net.send(v.at[0], rx.at[k], zs[k]) for k in range(3)]
+    yield
+    for h in hs:
+        h.wait_recv()
+    low = lax.broadcasted_iota(jnp.int32, (8, 256), 0) < 4
+    v[1] = v[0] + jnp.where(low, 0.0, rx[0] + rx[1] + rx[2])
+    for i, dev in ((1, coredev), (2, yldev), (3, yhd)):
+        h = net.send(v.at[i], rx.at[2 + i], dev)
+        yield
+        h.wait_recv()
+        v[i + 1] = v[i] + rx[2 + i]
+    hs = [net.send(v.at[4], rx.at[6 + k], xs[k]) for k in range(3)]
+    yield
+    for h in hs:
+        h.wait_recv()
+    v[5] = v[4] + rx[6] + rx[7] + rx[8]
+
+
+def step(*gens):
+    for g in gens:
+        next(g, None)
+
+
+def finish(*gens):
+    live = list(gens)
+    done = object()
+    while live:
+        live = [g for g in live if next(g, done) is not done]
+
+
+def attn_bwd_kernel(gmid_ref, oall_hbm, w_ref, q_ref, kv_ref, mix_ref, ln_ref, lat_ref, rlat_ref, qu_hbm, ld_ref,
+                    kvw_ref, x_ref, cos_ref, sin_ref, ig_ref, lg_ref, gmg_ref, ggu_ref, gdn_ref,
+                    gx_ref, fgu_ref, fdn_ref, fout_ref, fqu_ref, fld_ref, vec_ref,
+                    oall_ref, qu_v, gb, gmx, gqr, acc, kvt, kvrx, glt, glrx, glat, st_tx, st_rx,
+                    gocrx, goyrx, pqu, pld, vec, vrx,
+                    utx, urx, ub, uprx, upc, dtx, drx, db, dprx, dpc, otx, orx, ob, oprx,
+                    qcrx, qcs, qtx, qrx, qb, qyrx, qb2, qprx, lcrx, lcs, ltx, lrx, lb, lyrx, lb2, lprx,
+                    ssem, rsem, lsem):
+    r, c, coredev, yldev, zs = place()
+    x, xs = x_peers()
+    p = lax.axis_index("dp")
+    yh, yhd = p // 4, {"dp": lax.rem(p + 4, 8)}
+    core, yl = lax.rem(c, 2), c // 2
+    at, at_all = (x, xs, yh, yhd), (x, xs, yh, yhd, core, coredev, yl, yldev)
+    others = [(j % 4, j // 4) for j in range(1, 16)]
+    group = [{"row": lax.rem(r + i, 4), "col": lax.rem(c + j, 4)} for i, j in others]
+    net = Links(ssem, rsem, lsem)
+    oall_in = net.local(oall_hbm, oall_ref)
+    qu_in = net.local(qu_hbm, qu_v)
+    gop, goytx, gosum = oall_ref.at[pl.ds(0, 2)], oall_ref.at[2], oall_ref.at[3]
+    gb[r] = gmid_ref[...].astype(BF)
+    meet(group + xs + [yhd])
+    got = [net.send(gb.at[r], gb.at[r], zs[k - 1]) for k in (2, 1, 3)]
+
+    def spread_to(pc, fin):
+        def spread(t, piece):
+            pc[...] = t.astype(BF)
+            hs = [net.send(pc.at[lax.rem(r + k, 4)], fin.at[r, piece], zs[k - 1]) for k in (2, 1, 3)]
+            fin[r, piece] = pc[r]
+            yield
+            for h in hs:
+                h.wait_recv()
+        return spread
+
+    red_u = reduce_dp(net, at, lambda j, h: ggu_ref.at[:, rows_of(j * 128 + h * 64, 64)], (utx, urx, ub, uprx),
+                      lambda rows: fgu_ref.at[:, rows], 64, spread_to(upc, fgu_ref))
+    red_d = reduce_dp(net, at, lambda j, h: gdn_ref.at[:, rows_of(j * 96 + h * 48, 48)], (dtx, drx, db, dprx),
+                      lambda rows: fdn_ref.at[:, rows], 48, spread_to(dpc, fdn_ref))
+    step(red_d, red_u)
+    oall_in.wait()
+    for g in got:
+        g.wait_recv()
+
+    def mixed_grad(h, carry):
+        t = jnp.zeros((256, 256), F32)
+        for k in range(4):
+            t = t + dot(gb[k], oall_ref[k, blk(h)], NT)
+        gmx[h] = t.astype(BF)
+        return carry
+
+    lax.fori_loop(0, 4, mixed_grad, 0)
+
+    def out_block(b, t):
+        return dot(mix_ref[:, blk(t)], gb[b], TN)
+
+    def to_core(t, carry):
+        for i in range(2):
+            b = lax.rem(c + 1 - 2 * core + 2 * i, 4)
+            gop[i, blk(t)] = out_block(b, t).astype(BF)
+        return carry
+
+    def from_core(t, carry):
+        goytx[blk(t)] = (out_block(lax.rem(c + 2, 4), t) + gocrx[1, blk(t)].astype(F32)).astype(BF)
+        gosum[blk(t)] = (out_block(c, t) + gocrx[0, blk(t)].astype(F32)).astype(BF)
+        return carry
+
+    def from_y(t, carry):
+        gosum[blk(t)] = (gosum[blk(t)].astype(F32) + goyrx[blk(t)].astype(F32)).astype(BF)
+        return carry
+
+    def reduce_out():
+        lax.fori_loop(0, 4, to_core, 0)
+        h = net.send(gop, gocrx, coredev)
+        yield
+        h.wait_recv()
+        lax.fori_loop(0, 4, from_core, 0)
+        h = net.send(goytx, goyrx, yldev)
+        yield
+        h.wait_recv()
+        lax.fori_loop(0, 4, from_y, 0)
+
+        def spread(t, piece):
+            fout_ref[piece] = t.astype(BF)
+            return
+            yield
+
+        yield from reduce_dp(net, at, lambda j, h: gosum.at[rows_of(j * 256 + h * 128, 128)], (otx, orx, ob, oprx),
+                             lambda rows: fout_ref.at[rows], 128, spread)
+
+    red_o = reduce_out()
+    step(red_o)
+
+    acc[...] = jnp.zeros_like(acc)
+
+    def head(h, carry):
+        gm = gmx[h]
+        gw = dot(gm, kv_ref[:, 256:], NT)
+        w = w_ref[h]
+        wf = w.astype(F32)
+        t = wf * gw
+        gs = (t - wf * jnp.sum(t, axis=1, keepdims=True)).astype(BF)
+        gq = dot(gs, kv_ref[:, :256]) * (1.0 / 16.0)
+        gqr[:, blk(h)] = unrope(gq, cos_ref[...], sin_ref[...]).astype(BF)
+        acc[:, :256] += dot(gs, q_ref[h], TN)
+        acc[:, 256:] += dot(w, gm, TN)
+        return carry
+
+    lax.fori_loop(0, 4, head, 0)
+    kvt[...] = acc[...].astype(BF)
+    kv_got = []
+    for i, (a, b) in enumerate(others):
+        rows = rows_of(lax.rem(c + b, 4) * 256 + lax.rem(r + a, 4) * 64, 64)
+        kv_got.append(net.send(kvt.at[rows], kvrx.at[i], group[i]))
+    qu_in.wait()
+
+    def latent_grad(t, carry):
+        glt[:, blk(t)] = dot(gqr[...], qu_v[blk(t)], NT).astype(BF)
+        return carry
+
+    lax.fori_loop(0, 4, latent_grad, 0)
+    gl_got = [net.send(glt.at[rows_of(lax.rem(r + k, 4) * 64, 64)], glrx.at[k - 1], zs[k - 1]) for k in (2, 1, 3)]
+    step(red_o)
+
+    def query_up_grad(t, carry):
+        pqu[blk(t)] = dot(ln_ref[:, :, blk(t)].reshape(256, 256), gqr[...], TN).astype(BF)
+        return carry
+
+    lax.fori_loop(0, 4, query_up_grad, 0)
+    red_q = reduce_all(net, at_all, pqu, (qcrx, qcs, qtx, qrx, qb, qyrx, qb2, qprx), fqu_ref)
+    step(red_q)
+
+    own = rows_of(r * 64, 64)
+    mine = acc[rows_of(c * 256 + r * 64, 64)]
+    for i, h in enumerate(kv_got):
+        h.wait_recv()
+        mine = mine + kvrx[i].astype(F32)
+    gl = glt[own].astype(F32)
+    for i, h in enumerate(gl_got):
+        h.wait_recv()
+    for k in range(3):
+        gl = gl + glrx[k].astype(F32)
+    lat, rl = lat_ref[...], rlat_ref[:, :1]
+    gained = gl * lg_ref[...]
+    glat[r, :, :1024] = (rl * gained - lat * (rl * rl * rl * jnp.mean(gained * lat, axis=1, keepdims=True))).astype(BF)
+    glat[r, :, 1024:1280] = unrope(mine[:, :256], cos_ref[own], sin_ref[own]).astype(BF)
+    glat[r, :, 1280:] = mine[:, 256:].astype(BF)
+    la_got = [net.send(glat.at[r], glat.at[r], zs[k - 1]) for k in (2, 1, 3)]
+    glg = jnp.sum(gl * lat * rl, axis=0, keepdims=True)
+    step(red_d, red_u, red_q)
+    for h in la_got:
+        h.wait_recv()
+    g_all = glat[...].reshape(256, 1536)
+    xf = x_ref[...].astype(F32)
+    r_in = unpack_stat(ln_ref[:, :, 1024:].reshape(256, 128))
+    gn = dot(g_all[:, :1024], ld_ref[...], NT) + dot(g_all[:, 1024:], kvw_ref[...], NT)
+    gained = gn * ig_ref[...]
+    stat = jnp.sum(gained * xf, axis=1, keepdims=True)
+    st_tx[...] = jnp.broadcast_to(stat, (256, 128))
+    st_got = [net.send(st_tx, st_rx.at[k - 1], zs[k - 1]) for k in (2, 1, 3)]
+    normed = (xf * r_in * ig_ref[...]).astype(BF)
+    pld[...] = dot(normed, g_all, TN).astype(BF)
+    red_l = reduce_all(net, at_all, pld, (lcrx, lcs, ltx, lrx, lb, lyrx, lb2, lprx), fld_ref)
+    step(red_l)
+    gig = jnp.sum(gn * xf * r_in, axis=0, keepdims=True)
+    for i in range(2):
+        vec[0, i:i + 1] = gig[:, 256 * i:256 * i + 256]
+        vec[0, 2 + i:3 + i] = gmg_ref[:, 256 * i:256 * i + 256]
+    for i in range(4):
+        vec[0, 4 + i:5 + i] = glg[:, 256 * i:256 * i + 256]
+    red_v = reduce_vec(net, at_all, zs, vec, vrx)
+    step(red_v)
+    for h in st_got:
+        h.wait_recv()
+    for k in range(3):
+        stat = stat + st_rx[k, :, :1]
+    gx_ref[...] = (gmid_ref[...] + r_in * gained - xf * (r_in * r_in * r_in * stat / D)).astype(BF)
+    finish(red_l, red_v, red_q, red_o, red_d, red_u)
+    vec_ref[...] = vec[5]
+    net.close()
+
+
+def attn_bwd(*args):
+    def ring(*shape):
+        return [pltpu.VMEM((2, *shape), BF), pltpu.VMEM((6, *shape), BF), pltpu.VMEM((2, *shape), BF),
+                pltpu.VMEM(shape, BF)]
+
+    def whole(half, lanes):
+        n = half // 8
+        return [pltpu.VMEM((half, lanes), BF), pltpu.VMEM((half, lanes), BF), *ring(n, lanes),
+                pltpu.VMEM((2, n // 2, lanes), BF), pltpu.VMEM((n // 2, lanes), BF)]
+
+    v = pltpu.VMEM
+    return pl.pallas_call(
+        attn_bwd_kernel,
+        out_shape=(S((256, 512)), S((4, 512, 768)), S((4, 384, 512)), S((1024, 512)), S((1024, 1024)),
+                   S((512, 1536)), S((8, 256), F32)),
+        in_specs=[VM, ANY] + [VM] * 7 + [ANY] + [VM] * 10,
+        out_specs=(VM,) * 7,
+        scratch_shapes=[
+            v((4, 1024, 512), BF), v((1024, 1024), BF), v((4, 256, 512), BF), v((4, 256, 256), BF), v((256, 1024), BF), v((1024, 512), F32),
+            v((1024, 512), BF), v((15, 64, 512), BF), v((256, 1024), BF), v((3, 64, 1024), BF), v((4, 64, 1536), BF),
+            v((256, 128), F32), v((3, 256, 128), F32),
+            v((2, 1024, 512), BF), v((1024, 512), BF),
+            v((1024, 1024), BF), v((512, 1536), BF), v((6, 8, 256), F32), v((9, 8, 256), F32),
+            *ring(4, 64, 768), v((4, 64, 768), BF), *ring(4, 48, 512), v((4, 48, 512), BF), *ring(128, 512),
+            *whole(512, 1024), *whole(256, 1536),
+            pltpu.SemaphoreType.DMA((144,)), pltpu.SemaphoreType.DMA((144,)), pltpu.SemaphoreType.DMA((2,))],
+        compiler_params=pltpu.CompilerParams(collective_id=2, has_side_effects=True, vmem_limit_bytes=62 << 20),
+        name="attn_bwd",
+    )(*args)
+
+
 def shards(tokens, documents, piece_starts, latent_down, key_value, query_up, output_weight, gate_weight, up_weight,
            down_weight, input_gain, latent_gain, middle_gain, cotangent):
     cos, sin = own_rope(256)
+    ig, lg, mg = input_gain[None], latent_gain[None], middle_gain[None]
     lnst, lat, rlat, q, kv, w, mix, oall, mid, nm, rmid, gu, dn, call = attn_fwd(
-        tokens, documents, piece_starts, latent_down, key_value, query_up, output_weight, input_gain[None],
-        latent_gain[None], middle_gain[None], cos, sin, cotangent, jnp.pad(gate_weight, ((0, 0), (0, 128))),
+        tokens, documents, piece_starts, latent_down, key_value, query_up, output_weight, ig, lg, mg, cos, sin,
+        cotangent, jnp.pad(gate_weight, ((0, 0), (0, 128))),
         jnp.pad(up_weight, ((0, 0), (0, 128))), jnp.pad(down_weight, ((0, 128), (0, 0))))
-    out, gmid, gain_mid, ggu, gdn = ffn(nm, gu, dn, call, mid, rmid, middle_gain[None])
-    a = lax.psum_scatter(ggu.reshape(4, 8, 64, 768), "dp", scatter_dimension=1)
-    b = lax.psum_scatter(gdn.reshape(4, 8, 48, 512), "dp", scatter_dimension=1)
-    a = lax.all_to_all(a, "row", 0, 0, tiled=True)
-    b = lax.all_to_all(b, "row", 0, 0, tiled=True)
-    a = jnp.moveaxis(a, 0, 1)
-    a = lax.all_gather(a, "dp", axis=0, tiled=True)
-    b = lax.all_gather(b, "dp", axis=1)
-    grad_gate = a[:, :, :384].reshape(512, 1536)[:, :1408].astype(F32)
-    grad_up = a[:, :, 384:].reshape(512, 1536)[:, :1408].astype(F32)
-    grad_down = b.reshape(1536, 512)[:1408].astype(F32)
-    r, c = lax.axis_index("row"), lax.axis_index("col")
-    gb = gmid.astype(BF)
-    gb_all = lax.all_gather(gb, "row", axis=0)
-    gmix = sum(jnp.dot(gb_all[k], oall[k].T, preferred_element_type=F32) for k in range(4)).astype(BF)
-    gout = jnp.einsum("tm,ktn->mkn", mix, gb_all, preferred_element_type=F32).reshape(1024, 2048)
-    gout = lax.psum_scatter(gout.astype(BF), "col", scatter_dimension=1, tiled=True)
-    gout = lax.psum(gout, "dp").astype(F32)
-    gmix = gmix.reshape(256, 4, 256)
-    keys, values = kv[:, :256], kv[:, 256:]
-    gw = jnp.einsum("qhd,kd->hqk", gmix, values, preferred_element_type=F32)
-    wf = w.astype(F32)
-    gs = (wf * (gw - jnp.sum(gw * wf, axis=2, keepdims=True))).astype(BF)
-    gq = jnp.einsum("hqk,kd->qhd", gs, keys, preferred_element_type=F32) / 16.0
-    gk = jnp.einsum("hqk,hqd->kd", gs, q, preferred_element_type=F32)
-    gv = jnp.einsum("hqk,qhd->kd", w, gmix, preferred_element_type=F32)
-
-    def un(g, cs, sn):
-        a, b = g[..., :128], g[..., 128:]
-        return jnp.concatenate([a * cs + b * sn, b * cs - a * sn], axis=-1)
-
-    gqr = un(gq, cos[:, None], sin[:, None]).reshape(256, 1024).astype(BF)
-    ln = lnst[:, :, :1024].reshape(256, 1024)
-    r_in = jnp.sum(lnst[:, :, 1024:1027].astype(F32), axis=2).reshape(256, 1)
-    gqu = jnp.dot(ln.T, gqr, preferred_element_type=F32)
-    gln = lax.psum_scatter(jnp.dot(gqr, query_up.T, preferred_element_type=F32).astype(BF), "row",
-                           scatter_dimension=0, tiled=True).astype(F32)
-    gkv = lax.psum_scatter(jnp.concatenate([gk, gv], axis=1).astype(BF), ("col", "row"),
-                           scatter_dimension=0, tiled=True).astype(F32)
-    cs, sn = lax.dynamic_slice_in_dim(cos, r * 64, 64, 0), lax.dynamic_slice_in_dim(sin, r * 64, 64, 0)
-    rl = rlat[:, :1]
-    gained = gln * latent_gain
-    glat = rl * gained - lat * (rl**3 * jnp.mean(gained * lat, axis=1, keepdims=True))
-    glg = jnp.sum(gln * lat * rl, axis=0)
-    glat = jnp.concatenate([glat, un(gkv[:, :256], cs, sn), gkv[:, 256:]], axis=1).astype(BF)
-    glat = lax.all_gather(glat, "row", axis=0, tiled=True)
-    x = tokens.astype(F32)
-    normed = (x * r_in * input_gain).astype(BF)
-    gld = jnp.dot(normed.T, glat, preferred_element_type=F32)
-    gn = jnp.dot(glat[:, :1024], latent_down.T, preferred_element_type=F32)
-    gn = gn + jnp.dot(glat[:, 1024:], key_value.T, preferred_element_type=F32)
-    gained = gn * input_gain
-    stat = lax.psum(jnp.sum(gained * x, axis=1, keepdims=True), "row")
-    gx = gmid + r_in * gained - x * (r_in**3 * stat / D)
-    gig = jnp.sum(gn * x * r_in, axis=0)
-    gld, gqu = lax.psum((gld.astype(BF), gqu.astype(BF)), ("dp", "col"))
-    gig, gmg = lax.psum((gig, gain_mid[0]), ("dp", "col"))
-    glg = lax.psum(glg, ("dp", "row", "col"))
-    return (out, gx.astype(BF), gld[:, :1024].astype(F32), gld[:, 1024:].astype(F32), gqu.astype(F32), gout,
-            grad_gate, grad_up, grad_down, gig, glg, gmg)
+    out, gmid, gain_mid, ggu, gdn = ffn(nm, gu, dn, call, mid, rmid, mg)
+    gx, fgu, fdn, fout, fqu, fld, vec = attn_bwd(
+        gmid, oall, w, q, kv, mix, lnst, lat, rlat, query_up, latent_down, key_value, tokens, cos, sin, ig, lg,
+        gain_mid, ggu, gdn)
+    wide = jnp.moveaxis(fgu, 0, 1)
+    return (out, gx, fld[:, :1024].astype(F32), fld[:, 1024:].astype(F32), fqu.astype(F32), fout.astype(F32),
+            wide[:, :, :384].reshape(512, 1536)[:, :1408].astype(F32),
+            wide[:, :, 384:].reshape(512, 1536)[:, :1408].astype(F32),
+            fdn.reshape(1536, 512)[:1408].astype(F32),
+            vec[0:2].reshape(512), vec[4:8].reshape(1024), vec[2:4].reshape(512))
 
 
 def solution(mesh):

time: 761 us -> 389 us (0.51)
  waiting for transfers between devices: 311 us -> 0 us
  Pallas kernels: 180 us -> 349 us
  blocking collectives: 167 us -> 0 us
  matrix products: 20.4 us -> 0 us
  local copies, waits for them, and re-layouts: 41.8 us -> 22 us
  between operations: 14.5 us -> 0.72 us
  other arithmetic: 24.4 us -> 16.2 us
    pallas_call x0 -> x1, Pallas kernels: none -> 170 us  [attn_bwd(): pl.pallas_call(attn_bwd_kernel, out_shape=(S((256, 512)), S((4, 512, 768)...]
    psum x3 -> x0, blocking collectives: 137 us -> none  [the longest x1 65.1 us: shards(): glg = lax.psum(glg, ('dp', 'row', 'col'))]
    psum x2 -> x0, waiting for transfers between devices: 124 us -> none  [the longest x1 124 us: shards(): gout = lax.psum(gout, 'dp').astype(F32)]
    reduce_scatter x3 -> x0, waiting for transfers between devices: 109 us -> none  [the longest x1 61.6 us: shards(): lax.psum_scatter(jnp.concatenate([gk, gv], axis=1).astype(BF), ('col', 'r...]
    all_gather x3 -> x0, waiting for transfers between devices: 77.7 us -> none  [the longest x1 56.1 us: shards(): a = lax.all_gather(a, 'dp', axis=0, tiled=True)]
    dot_general x14 -> x0, matrix products: 20.4 us -> none  [the longest x4 5.26 us: shards(): jnp.dot(gb_all[k], oall[k].T, preferred_element_type=F32)]
    all_to_all x2 -> x0, blocking collectives: 17.8 us -> none  [the longest x1 9.22 us: shards(): b = lax.all_to_all(b, 'row', 0, 0, tiled=True)]
    all_gather x1 -> x0, blocking collectives: 11.8 us -> none  [shards(): glat = lax.all_gather(glat, 'row', axis=0, tiled=True)]
  transfers between devices with their start and end apart: 8 -> 0, of which waited for: 6 -> 0; matrix products, arithmetic and copies ran while one was open for 6% -> 0% of each run, Pallas kernels for 0% -> 0%
where the time goes in v2:
time: 389 us; the launch traced here: 388 us
  Pallas kernels  349 us (90%)
  local copies, waits for them, and re-layouts  22 us (6%)
  other arithmetic  16.2 us (4%)
    pallas_call x1, Pallas kernels, attn_bwd(): pl.pallas_call(attn_bwd_kernel, out_shape=(S((256, 512)), S((4, 512, 768)...  170 us
    pallas_call x1, Pallas kernels, attn_fwd(): pl.pallas_call(attn_fwd_kernel, out_shape=(S((4, 64, 1152)), S((64, 1024)...  94.8 us
    pallas_call x1, Pallas kernels, ffn(): pl.pallas_call(ffn_kernel, out_shape=(S((256, 512)), S((256, 512), F32),...  84.8 us
    unnamed x25, local copies, waits for them, and re-layouts  11 us

profile of v2, /device:TPU:1, one launch (start us, length us, event | category | flops | bytes accessed | tf_op | source)
XLA Modules:
  0.0 388.3 jit_solution(11894010598072340010)
XLA Ops:
  0.7 1.2 multiply_sine_fusion
  1.9 0.0 copy-start.2
  1.9 2.7 pad.11.gate_hbm
  4.6 0.0 copy-done.2
  4.6 0.0 copy-start.3
  4.6 1.3 pad.12.up_hbm
  5.9 0.7 copy-done.3
  6.6 1.2 pad.13.down_hbm
  7.8 94.8 %attn_fwd.1 = (bf16[4,64,1152]{2,1,0:T(8,128)(2,1)}, f32[64,1024]{1,0:T(8,128)}, f32[64,128]{1,0:T(8,128)}, bf16[4,256,256]{2,1,0:T(8,128)(2,1)}, bf16[1024,512]...) custom-call(bf16[256,512]{1,0:T(8,128)(2,1)} %x_ref.3, ...), custom_call_target="tpu_custom_call" | custom-call | tf_op jit(solution)/shard_map/attn_fwd/pallas_call | solution.py:388
  102.7 84.8 %ffn.1 = (bf16[256,512]{1,0:T(8,128)(2,1)}, f32[256,512]{1,0:T(8,128)}, f32[1,512]{1,0:T(1,128)}, bf16[4,512,768]{2,1,0:T(8,128)(2,1)}, bf16[4,384,512]{2,1,0:T(8,128)(2,1)}) custom-call(bf16[256,512]{1,0:T(8,128)(2,1)} %get-tuple-element.38.nm_ref, bf16[4,512,768]{2,1,0:T(8,128)(2,1)} %get-tuple-element.39.gu_ref, ...), custom_call_target="tpu_custom_call" | custom-call | tf_op jit(solution)/shard_map/ffn/pallas_call | solution.py:478
  187.5 169.7 %attn_bwd.1 = (bf16[256,512]{1,0:T(8,128)(2,1)}, bf16[4,512,768]{2,1,0:T(8,128)(2,1)}, bf16[4,384,512]{2,1,0:T(8,128)(2,1)}, bf16[1024,512]{1,0:T(8,128)(2,1)}, ...) custom-call(f32[256,512]{1,0:T(8,128)} %get-tuple-element.45.gmid_ref, ...), custom_call_target="tpu_custom_call" | custom-call | tf_op jit(solution)/shard_map/attn_bwd/pallas_call | solution.py:816
  357.2 0.0 copy-start.1
  357.2 0.8 slice_bitcast_fusion
  358.1 0.8 slice_bitcast_fusion.1
  358.8 0.6 copy.32
  359.4 0.6 copy.31
  360.0 0.6 copy.30
  360.6 2.1 slice_convert_fusion.4
  362.7 0.0 copy-done.1
  362.7 0.0 copy-start.5
  362.7 1.6 slice_convert_fusion.3
  364.3 0.0 copy-done.5
  364.3 0.0 copy-start.4
  364.3 1.6 convert_element_type.37
  366.0 0.2 copy-done.4
  366.1 0.0 copy-start
  366.2 2.0 slice_convert_fusion
  368.1 1.0 copy-done
  369.1 1.5 fusion
  370.6 1.6 copy.27
  372.2 1.8 slice_convert_fusion.1
  374.0 2.2 copy.29
  376.2 2.6 copy.26
  378.8 1.8 slice_convert_fusion.2
  380.5 2.2 copy.28
  382.7 0.0 copy-start.6
  382.8 0.0 copy-start.7
  382.8 4.1 %convert_element_type.36 = f32[1024,1024]{1,0:T(8,128)} convert(bf16[1024,1024]{1,0:T(8,128)(2,1)} %get-tuple-element.59) | non-fusion elementwise | flops 1048576 | bytes 6291456 | tf_op jit(solution)/shard_map/convert_element_type | solution.py:849
  386.9 0.0 copy-done.6
  386.9 0.7 copy.35
  387.6 0.0 copy-done.7
  387.6 0.7 copy.36
  (2 shorter events, 0.0 us)
Async XLA Ops:
  1.9 2.7 copy-start.2
  4.6 1.9 copy-start.3
  357.2 5.5 %copy-start.1 = (bf16[512,1536]{1,0:T(8,128)(2,1)S(1)}, bf16[512,1536]{1,0:T(8,128)(2,1)}, u32[]{:S(2)}) copy-start(bf16[512,1536]{1,0:T(8,128)(2,1)} %get-tuple-element.58) | copy-start | bytes 4718596
  362.7 1.6 copy-start.5
  364.3 1.8 copy-start.4
  366.1 2.9 copy-start
  382.7 4.1 %copy-start.6 = (bf16[256,512]{1,0:T(8,128)(2,1)S(1)}, bf16[256,512]{1,0:T(8,128)(2,1)}, u32[]{:S(2)}) copy-start(bf16[256,512]{1,0:T(8,128)(2,1)} %get-tuple-element.94) | copy-start | bytes 786436
  382.8 4.8 %copy-start.7 = (bf16[256,512]{1,0:T(8,128)(2,1)S(1)}, bf16[256,512]{1,0:T(8,128)(2,1)}, u32[]{:S(2)}) copy-start(bf16[256,512]{1,0:T(8,128)(2,1)} %get-tuple-element.95) | copy-start | bytes 786436
